TPU v7x, 256 devices: a whole 4x4x8 slice. The times are simulated.
256 devices in a mesh: cam: 8 (over x, core), clip: 32 (over y, z).
Axes of the slice: x: 4, y: 4, z: 8, core: 2. Of those that a mesh axis runs over, the one named last changes fastest.
Arguments:
- tokens: bfloat16 [64, 8, 256, 1024], P('clip', 'cam'), may hold values from -6 to 6
- w_query: bfloat16 [1024, 1024], replicated, may hold values from -0.1875 to 0.1875
- w_key: bfloat16 [1024, 1024], replicated, may hold values from -0.1875 to 0.1875
- w_value: bfloat16 [1024, 1024], replicated, may hold values from -0.1875 to 0.1875
- w_proj: bfloat16 [1024, 256], replicated, may hold values from -0.1875 to 0.1875
- prototypes: bfloat16 [256, 65536], P(None, ('cam', 'clip')), may hold values from -6 to 6
Outputs:
- codes: float32 [64, 65536], P(None, ('cam', 'clip'))
- prototype_gradient: float32 [256, 65536], P(None, ('cam', 'clip'))
- grad_proj: float32 [1024, 256], P('clip')
- grad_value: float32 [1024, 1024], P('clip', 'cam')
All inputs are finite; a program needn't handle non-finite values.
Results may differ from a plain program's by a relative error of at most 0.015.
Values may be sent and summed in bfloat16 or wider, within the bound.
A program may use at most 128 MiB of HBM per device.

v0:
```python
import jax
import jax.numpy as jnp
from jax import lax
from jax.sharding import PartitionSpec as P

D = 1024
HD = 64
PROTOS = 65536
TOK = 256
ITERS = 3
H = 16


SINK_EPS = 0.05
SOFTMAX_TEMP = 0.1
NORM_EPS = 1e-06
heads_per_group = 4


def column_sums(query_rows, key_rows, total):
    scores = jnp.einsum(
        "ihe,jhe->hij", query_rows, key_rows, preferred_element_type=jnp.float32
    ) * HD ** (-0.5)
    exponent_values = jnp.exp(scores)
    probs = exponent_values / jnp.sum(exponent_values, axis=2, keepdims=True)
    return jnp.sum(probs, axis=1) / total


def camera_block(query_clip, key_clip, total):
    tokens_here = query_clip.shape[0]
    width = heads_per_group * HD
    parts = []
    for group in range(H // heads_per_group):
        query_group = query_clip[:, group * width : (group + 1) * width].reshape(
            tokens_here, heads_per_group, HD
        )
        key_group = key_clip[:, group * width : (group + 1) * width].reshape(
            total, heads_per_group, HD
        )
        parts.append(column_sums(query_group, key_group, total))
    return jnp.concatenate(parts, axis=0)


def local(tokens, w_query, w_key, w_value, w_proj, prototypes):
    clips = tokens.shape[0]
    own = tokens.reshape(clips, TOK, D)
    query_vectors = jnp.einsum(
        "ctd,de->cte", own, w_query, preferred_element_type=jnp.float32
    ).astype(jnp.bfloat16)
    key_rows = jnp.einsum("ctd,de->cte", own, w_key, preferred_element_type=jnp.float32).astype(
        jnp.bfloat16
    )
    collected_rows = lax.all_gather(key_rows.reshape(clips, 1, TOK, D), "cam", axis=1, tiled=True)
    cameras = collected_rows.shape[1]
    total = cameras * TOK

    def per_clip(clip_pair):
        return camera_block(clip_pair[0], clip_pair[1], total)

    partial_sums = lax.map(per_clip, (query_vectors, collected_rows.reshape(clips, total, D)))
    weights = lax.psum_scatter(
        partial_sums.reshape(clips, H, cameras, TOK), "cam", scatter_dimension=2, tiled=True
    )
    weights = weights.reshape(clips, H, TOK).astype(jnp.bfloat16)
    mixture = jnp.einsum("chj,cjd->chd", weights, own, preferred_element_type=jnp.float32).astype(
        jnp.bfloat16
    )
    head_out = jnp.einsum(
        "chd,dhe->che", mixture, w_value.reshape(D, H, HD), preferred_element_type=jnp.float32
    )
    pooled = lax.psum(head_out.reshape(clips, D), "cam").astype(jnp.bfloat16)
    share_rows = D // lax.axis_size("clip")
    embed = jnp.dot(pooled, w_proj, preferred_element_type=jnp.float32)
    embed_norm = jnp.sqrt(jnp.sum(embed * embed, axis=1, keepdims=True) + NORM_EPS)
    unit = embed / embed_norm
    unit_b = unit.astype(jnp.bfloat16)
    all_units = lax.all_gather(unit_b, "clip", axis=0, tiled=True)
    proto_f = prototypes.astype(jnp.float32)
    column_norm = jnp.sqrt(jnp.sum(proto_f * proto_f, axis=0, keepdims=True) + NORM_EPS)
    unit_proto = proto_f / column_norm
    proto_b = unit_proto.astype(jnp.bfloat16)
    logit_scores = jnp.dot(all_units, proto_b, preferred_element_type=jnp.float32)
    exponent_values = jnp.exp(logit_scores / SOFTMAX_TEMP)
    assign = jnp.exp(logit_scores / SINK_EPS)
    prob_total = lax.psum(jnp.sum(exponent_values, axis=1), ("cam", "clip"))
    first_step = 0
    for step in range(first_step, ITERS):
        assign = assign / jnp.sum(assign, axis=0, keepdims=True)
        row_total = lax.psum(jnp.sum(assign, axis=1), ("cam", "clip"))
        assign = assign / row_total[:, None]
    prob = exponent_values / prob_total[:, None]
    grad_logits = (PROTOS * (prob - assign)).astype(jnp.bfloat16)
    codes = PROTOS * assign
    grad_unit = lax.psum_scatter(
        jnp.dot(grad_logits, proto_b.T, preferred_element_type=jnp.float32),
        "clip",
        scatter_dimension=0,
        tiled=True,
    )
    grad_unit = lax.psum(grad_unit, "cam")
    grad_embed = (grad_unit - unit * jnp.sum(unit * grad_unit, axis=1, keepdims=True)) / embed_norm
    grad_embed_b = grad_embed.astype(jnp.bfloat16)
    grad_pooled = jnp.dot(grad_embed_b, w_proj.T, preferred_element_type=jnp.float32).astype(
        jnp.bfloat16
    )
    piece = pooled
    grad_proj = lax.psum_scatter(
        jnp.einsum("cd,ce->de", piece, grad_embed_b, preferred_element_type=jnp.float32),
        "clip",
        scatter_dimension=0,
        tiled=True,
    )
    grad_heads = grad_pooled.reshape(clips, H, HD)
    piece = lax.slice_in_dim(mixture, 0, share_rows * lax.axis_size("clip"), axis=2)
    value_rows = lax.psum_scatter(
        jnp.einsum("chd,che->dhe", piece, grad_heads, preferred_element_type=jnp.float32).reshape(
            share_rows * lax.axis_size("clip"), D
        ),
        "clip",
        scatter_dimension=0,
        tiled=True,
    )
    grad_value = lax.psum_scatter(value_rows, "cam", scatter_dimension=1, tiled=True)
    grad_unit_proto = jnp.einsum(
        "be,bk->ek", all_units, grad_logits, preferred_element_type=jnp.float32
    )
    prototype_gradient = (
        grad_unit_proto - unit_proto * jnp.sum(unit_proto * grad_unit_proto, axis=0, keepdims=True)
    ) / column_norm
    return (codes, prototype_gradient, grad_proj, grad_value)


def solution(mesh):
    in_specs = (P("clip", "cam", None, None), P(), P(), P(), P(), P(None, ("cam", "clip")))
    out_specs = (
        P(None, ("cam", "clip")),
        P(None, ("cam", "clip")),
        P("clip", None),
        P("clip", "cam"),
    )
    return jax.shard_map(local, mesh=mesh, in_specs=in_specs, out_specs=out_specs, check_vma=False)
```

profile of v0, /device:TPU:1, one launch (start us, length us, event | category | flops | bytes accessed | tf_op | source)
XLA Modules:
  0.0 1158.2 jit_solution(2229369669846176685)
XLA Ops:
  20.2 48.7 %all-gather.4.cloned.1.call-done = bf16[2,2048,1024]{2,1,0:T(8,128)(2,1)} async-done(((bf16[2,256,1024]{2,1,0:T(8,128)(2,1)}), bf16[2,2048,1024]{2,1,0:T(8,128)(2,1)}) %all-gather.4.cloned.1.call-update) | async-done | bytes 8388624 | tf_op jit(solution)/shard_map/all_gather | solution.py:53
  68.9 130.2 %while.10 = (s32[]{:T(128)}, f32[2,16,2048]{2,1,0:T(8,128)}, bf16[2,256,1024]{2,1,0:T(8,128)(2,1)}, bf16[2,2048,1024]{2,1,0:T(8,128)(2,1)}, s32[]{:T(128)}) while((s32[]{:T(128)}, f32[2,16,2048]{2,1,0:T(8,128)}, bf16[2,256,1024]{2,1,0:T(8,128)(2,1)}, bf16[2,2048,1024]{2,1,0:T(8,128)(2,1)}, s32[]{:T(128)}) %tuple.47), condition=%wide.region_9.10_spmd, body=%wide.region_0.9_spmd.sunk | while | flops 2181148672 | bytes 112328888 | solution.py:60
  73.5 6.5 copy.50
  88.5 5.7 fusion.143
  94.2 7.5 divide_reduce_fusion.11
  106.2 6.1 divide_reduce_fusion.12
  117.6 5.5 divide_reduce_fusion.10
  127.6 5.6 divide_reduce_fusion.9
  138.6 6.5 copy.50
  153.6 5.7 fusion.143
  159.3 7.5 divide_reduce_fusion.11
  171.3 6.1 divide_reduce_fusion.12
  192.7 5.6 divide_reduce_fusion.9
  202.8 29.3 %reduce-scatter.5.cloned.1.call-done = f32[2,16,1,256]{3,1,0,2:T(8,128)} async-done(((f32[2,16,8,256]{3,1,0,2:T(8,128)}), f32[2,16,1,256]{3,1,0,2:T(8,128)}) %reduce-scatter.5.cloned.1.call-update) | async-done | bytes 32784 | tf_op jit(solution)/shard_map/reduce_scatter | solution.py:61
  235.9 14.8 %psum.42 = bf16[2,1024]{1,0:T(2,128)(2,1)S(1)} all-reduce(f32[2,1024]{1,0:T(2,128)S(1)} %reshape.88), channel_id=1, replica_groups=mesh['cam'=8,'clip'=32] {'cam'}, use_global_device_ids=true, to_apply=%region_11.12 | all-reduce | flops 2048 | bytes 12288 | tf_op jit(solution)/shard_map/psum | solution.py:71
  252.1 33.8 %all-gather.1 = bf16[32,2,256]{2,1,0:T(2,128)(2,1)S(1)} all-gather(bf16[1,2,256]{2,1,0:T(2,128)(2,1)S(1)} %get-tuple-element.51), channel_id=1, replica_groups=mesh['cam'=8,'clip'=32] {'clip'}, dimensions={0}, use_global_device_ids=true | all-gather | bytes 33792 | tf_op jit(solution)/shard_map/all_gather | solution.py:77
  286.2 84.4 %psum.43 = f32[64]{0:T(128)S(1)} all-reduce(f32[64]{0:T(128)S(1)} %get-tuple-element.40), channel_id=1, replica_groups=mesh['cam'=8,'clip'=32] {'cam','clip'}, use_global_device_ids=true, to_apply=%region_16.17 | all-reduce | flops 64 | bytes 512 | tf_op jit(solution)/shard_map/psum | solution.py:89
  370.9 72.8 %psum.44 = f32[64]{0:T(128)S(1)} all-reduce(f32[64]{0:T(128)S(1)} %fusion.48), channel_id=1, replica_groups=mesh['cam'=8,'clip'=32] {'cam','clip'}, use_global_device_ids=true, to_apply=%region_19.20 | all-reduce | flops 64 | bytes 512 | tf_op jit(solution)/shard_map/psum | solution.py:89
  444.0 73.4 %all-reduce.1 = (f32[64]{0:T(128)S(1)}, f32[64]{0:T(128)S(1)}) all-reduce(f32[64]{0:T(128)S(1)} %fusion.50, f32[64]{0:T(128)S(1)} %get-tuple-element.39), channel_id=1, replica_groups=mesh['cam'=8,'clip'=32] {'cam','clip'}, use_global_device_ids=true, to_apply=%region_22.23 | all-reduce | flops 128 | bytes 1024 | tf_op jit(solution)/shard_map/psum | solution.py:89
  520.3 132.7 %all-reduce.4.cloned.1.call-done = f32[64,256]{1,0:T(8,128)} async-done(((f32[64,256]{1,0:T(8,128)}), f32[64,256]{1,0:T(8,128)}) %all-reduce.4.cloned.1.call-update) | async-done | bytes 65552
  653.7 16.7 %psum.47 = f32[2,256]{1,0:T(2,128)S(1)} all-reduce(f32[2,256]{1,0:T(2,128)S(1)} %constant_dynamic-slice_fusion.2), channel_id=1, replica_groups=mesh['cam'=8,'clip'=32] {'cam'}, use_global_device_ids=true, to_apply=%region_27.28 | all-reduce | flops 512 | bytes 4096 | tf_op jit(solution)/shard_map/psum | solution.py:100
  681.5 213.6 %reduce-scatter.9.cloned.1.call-done = f32[32,1024]{1,0:T(8,128)} async-done(((f32[1024,1024]{1,0:T(8,128)}), f32[32,1024]{1,0:T(8,128)}) %reduce-scatter.9.cloned.1.call-update) | async-done | bytes 131088 | tf_op jit(solution)/shard_map/reduce_scatter | solution.py:115
  896.1 217.6 %reduce-scatter.7.cloned.1.call-done = f32[32,256]{1,0:T(8,128)} async-done(((f32[1024,256]{1,0:T(8,128)}), f32[32,256]{1,0:T(8,128)}) %reduce-scatter.7.cloned.1.call-update) | async-done | bytes 32784 | tf_op jit(solution)/shard_map/reduce_scatter | solution.py:107
  1113.8 37.6 %reduce-scatter.11.cloned.1.call-done = f32[32,128]{1,0:T(8,128)} async-done(((f32[32,1024]{1,0:T(8,128)}), f32[32,128]{1,0:T(8,128)}) %reduce-scatter.11.cloned.1.call-update) | async-done | bytes 16400 | tf_op jit(solution)/shard_map/reduce_scatter | solution.py:123
  (95 shorter events, 99.5 us)
Async XLA Ops:
  7.2 1.6 copy-start
  7.2 9.2 copy-start.5
  7.2 61.7 %all-gather.4.cloned.1.call-start = ((), (), s32[]{:S(2)}) async-start(), calls=%async_computation.8 | async-start | bytes 9437184 | tf_op jit(solution)/shard_map/all_gather | solution.py:53
  12.3 219.7 %reduce-scatter.5.cloned.1.call-start = ((), (), s32[]{:S(2)}) async-start(), calls=%async_computation.4 | async-start | bytes 294912 | tf_op jit(solution)/shard_map/reduce_scatter | solution.py:61
  68.9 450.2 %copy-start.8 = (u32[256]{0:T(256)S(1)}, u32[256]{0:T(256)}, u32[]{:S(2)}) copy-start(u32[256]{0:T(256)} %constant.40) | copy-start | bytes 3076
  79.9 3.8 copy-start.3
  87.8 0.6 copy-start.2
  127.6 5.6 copy-start.6
  133.3 0.7 copy-start.7
  145.0 3.8 copy-start.3
  152.9 0.6 copy-start.2
  192.7 5.6 copy-start.6
  198.4 0.7 copy-start.7
  200.8 452.2 %all-reduce.4.cloned.1.call-start = ((), (), s32[]{:S(2)}) async-start(), calls=%async_computation.9 | async-start | bytes 131072
  519.0 376.1 %reduce-scatter.9.cloned.1.call-start = ((), (), s32[]{:S(2)}) async-start(), calls=%async_computation.6 | async-start | bytes 4325376 | tf_op jit(solution)/shard_map/reduce_scatter | solution.py:115
  671.9 479.5 %copy-start.1 = (bf16[1024,1024]{1,0:T(8,128)(2,1)S(1)}, bf16[1024,1024]{1,0:T(8,128)(2,1)}, u32[]{:S(2)}) copy-start(bf16[1024,1024]{1,0:T(8,128)(2,1)} %param.10) | copy-start | bytes 6291460
  674.7 220.5 %copy-start.4 = (bf16[256,256]{1,0:T(8,128)(2,1)S(1)}, bf16[256,256]{1,0:T(8,128)(2,1)}, u32[]{:S(2)}) copy-start(bf16[256,256]{1,0:T(8,128)(2,1)} %param.13) | copy-start | bytes 393220
  680.1 433.7 %reduce-scatter.7.cloned.1.call-start = ((), (), s32[]{:S(2)}) async-start(), calls=%async_computation.5 | async-start | bytes 1081344 | tf_op jit(solution)/shard_map/reduce_scatter | solution.py:107
  681.5 469.9 %reduce-scatter.11.cloned.1.call-start = ((), (), s32[]{:S(2)}) async-start(), calls=%async_computation.7 | async-start | bytes 147456 | tf_op jit(solution)/shard_map/reduce_scatter | solution.py:123
Sparse Core Ops, SparseCore 0:
  12.5 56.3 all-gather.3
  200.9 31.0 reduce-scatter.4
  519.1 133.8 all-reduce.3
  680.2 214.8 reduce-scatter.8
  899.3 214.3 reduce-scatter.6
  1116.7 34.6 reduce-scatter.10
where the time goes:
time: 1160 us
  waiting for transfers between devices  680 us (59%)
  blocking collectives  296 us (26%)
  matrix products  107 us (9%)
  local copies, waits for them, and re-layouts  54.6 us (5%)
  between operations  14.9 us (1%)
    psum x3, blocking collectives, local(): row_total = lax.psum(jnp.sum(assign, axis=1), ('cam', 'clip'))  231 us
    reduce_scatter x1, waiting for transfers between devices, local(): lax.psum_scatter(jnp.einsum('cd,ce->de', piece, grad_embed_b, preferred_e...  218 us
    reduce_scatter x1, waiting for transfers between devices, local(): lax.psum_scatter(jnp.einsum('chd,che->dhe', piece, grad_heads, preferred_...  214 us
    unnamed x7, waiting for transfers between devices  133 us
    div x8, matrix products, column_sums(): probs = exponent_values / jnp.sum(exponent_values, axis=2, keepdims=True)  49.5 us
    all_gather x1, waiting for transfers between devices, local(): lax.all_gather(key_rows.reshape(clips, 1, TOK, D), 'cam', axis=1, tiled=T...  48.7 us
    dot_general x8, matrix products, column_sums(): jnp.einsum('ihe,jhe->hij', query_rows, key_rows, preferred_element_type=j...  38.4 us
    reduce_scatter x1, waiting for transfers between devices, local(): lax.psum_scatter(value_rows, 'cam', scatter_dimension=1, tiled=True)  37.6 us
  transfers between devices with their start and end apart: 6, of which 6 were waited for; matrix products, arithmetic and copies ran while one was open for 1% of the time, Pallas kernels for 0%

commit v1 on v0

v1 whole, which is shorter than its diff:
```python
import functools

import jax
import jax.numpy as jnp
from jax import lax
from jax.experimental import pallas as pl
from jax.experimental.pallas import tpu as pltpu
from jax.sharding import PartitionSpec as P

D = 1024
HD = 64
H = 16
BOT = 256
PROTOS = 65536
TOK = 256
CLIPS = 64
N_CAM = 8
N_CLIP = 32
N_Z = 8
N_Y = N_CLIP // N_Z
N_R = N_CAM * N_Y
PAIR = 2
LANES = 128
COLS = PROTOS // (N_CAM * N_CLIP)
SHARE = D // N_CLIP
KEYS = N_CAM * TOK
ROWS_AT_ONCE = 1024

SINK_EPS = 0.05
SOFTMAX_TEMP = 0.1
NORM_EPS = 1e-06
LOG2_E = 1.4426950408889634

MESH = pl.DeviceIdType.MESH
F32 = jnp.float32
BF16 = jnp.bfloat16


def dot(a, b, dims):
    return lax.dot_general(a, b, (dims, ((), ())), preferred_element_type=F32)


NN = ((1,), (0,))
NT = ((1,), (1,))
TN = ((0,), (0,))


def fold(a):
    return a[:, :LANES] + a[:, LANES:]


def twice(a):
    return jnp.concatenate([a, a], axis=1)


def kernel(
    x_in, wq_in, wk_in, wv_in, wp_in, pr_in,
    codes_out, proto_out, proj_out, value_out,
    xv, wq, wk, wv, wp, pr,
    proto_all, qk_send, qk_recv, acc,
    w_send, w_recv, mix_send, mix_recv, pool_send, pool_recv,
    z_send, z_recv, side_send, side_recv,
    a_buf, p_buf, v_buf, g_buf, unit_buf, norm_buf,
    row_send, row_recv, gu_send, gu_recv, gz_send, gz_recv,
    proj_tmp, value_tmp,
    load_sem, own_sem, qk_ss, qk_rs, cam_ss, cam_rs, proto_ss, proto_rs, wide_ss, wide_rs,
):
    cam = lax.axis_index("cam")
    clip = lax.axis_index("clip")
    y, z = lax.div(clip, N_Z), lax.rem(clip, N_Z)
    here = y * N_CAM + cam

    loads = [
        pltpu.make_async_copy(x_in, xv, load_sem.at[0]),
        pltpu.make_async_copy(wq_in, wq, load_sem.at[1]),
        pltpu.make_async_copy(wk_in, wk, load_sem.at[2]),
        pltpu.make_async_copy(pr_in, pr, load_sem.at[3]),
        pltpu.make_async_copy(wv_in, wv, load_sem.at[4]),
        pltpu.make_async_copy(wp_in, wp, load_sem.at[5]),
    ]
    for load in loads:
        load.start()

    def cam_peer(o):
        return (lax.rem(cam + o, N_CAM), clip)

    def clip_peer(o):
        return (cam, lax.rem(clip + o, N_CLIP))

    def z_peer(o):
        return (cam, y * N_Z + lax.rem(z + o, N_Z))

    def r_peer(o):
        other = lax.rem(here + o, N_R)
        return (lax.rem(other, N_CAM), lax.div(other, N_CAM) * N_Z + z)

    def loop(lo, hi, step):
        def body(i, carry):
            step(i)
            return carry

        lax.fori_loop(lo, hi, body, 0)

    barrier = pltpu.get_barrier_semaphore()

    def greet(device):
        pl.semaphore_signal(barrier, inc=1, device_id=device, device_id_type=MESH)

    loop(1, N_CAM, lambda o: greet(cam_peer(o)))
    loop(1, N_CLIP, lambda o: greet(clip_peer(o)))

    def greet_rest(i):
        oc, oy = 1 + lax.div(i, N_Y - 1), 1 + lax.rem(i, N_Y - 1)
        greet((lax.rem(cam + oc, N_CAM), lax.rem(y + oy, N_Y) * N_Z + z))

    rest = (N_CAM - 1) * (N_Y - 1)
    loop(0, rest, greet_rest)

    def project(b):
        rows = xv[b * TOK : (b + 1) * TOK, :]
        for which, weight in enumerate((wq, wk)):
            for j in range(D // 256):
                got = dot(rows, weight[:, j * 256 : (j + 1) * 256], NN).astype(BF16)
                qk_send[b, 2 * j, which] = got[:, :LANES]
                qk_send[b, 2 * j + 1, which] = got[:, LANES:]

    def qk_copy(b, o):
        to = cam_peer(o)
        return pltpu.make_async_remote_copy(
            src_ref=qk_send.at[b, to[0]], dst_ref=qk_recv.at[b, cam],
            send_sem=qk_ss.at[b, o], recv_sem=qk_rs.at[b, o],
            device_id=to, device_id_type=MESH,
        )

    def own_copy(b):
        return pltpu.make_async_copy(qk_send.at[b, cam], qk_recv.at[b, cam], own_sem.at[b])

    def proto_copy(o):
        return pltpu.make_async_remote_copy(
            src_ref=proto_all.at[z], dst_ref=proto_all.at[z],
            send_sem=proto_ss.at[o], recv_sem=proto_rs.at[o],
            device_id=z_peer(o), device_id_type=MESH,
        )

    for load in loads[:3]:
        load.wait()
    project(0)
    pl.semaphore_wait(barrier, N_CAM - 1 + N_CLIP - 1 + rest)
    loop(1, N_CAM, lambda o: qk_copy(0, o).start())
    own_copy(0).start()
    project(1)
    loop(1, N_CAM, lambda o: qk_copy(1, o).start())
    own_copy(1).start()

    loads[3].wait()
    proto = pr[...].astype(F32)
    col_norm = jnp.sqrt(jnp.sum(proto * proto, axis=0, keepdims=True) + NORM_EPS)
    proto_all[z] = (proto / col_norm).astype(BF16)
    loop(1, N_Z, lambda o: proto_copy(o).start())

    acc[...] = jnp.zeros_like(acc)
    cams_at_once = ROWS_AT_ONCE // TOK
    lane_q = lax.broadcasted_iota(jnp.int32, (ROWS_AT_ONCE, LANES), 1)

    def attend(b):
        loop(1, N_CAM, lambda o: qk_copy(b, o).wait_recv())
        own_copy(b).wait()

        def block(i):
            head, part = lax.div(i, N_CAM // cams_at_once), lax.rem(i, N_CAM // cams_at_once)
            keys = qk_recv[b, :, 1].reshape(KEYS, LANES)
            rows = qk_recv[b, pl.ds(part * cams_at_once, cams_at_once), 0].reshape(ROWS_AT_ONCE, LANES)
            rows = jnp.where(lax.div(lane_q, HD) == head, rows, jnp.zeros_like(rows))
            weights = jnp.exp2(dot(rows, keys, NT) * (HD ** (-0.5) * LOG2_E))
            weights = weights * (1.0 / jnp.sum(weights, axis=1, keepdims=True))
            acc[b * PAIR + head] += jnp.sum(weights.reshape(ROWS_AT_ONCE // 8, 8, KEYS), axis=0)

        loop(0, PAIR * N_CAM // cams_at_once, block)

    loop(0, PAIR, attend)

    def cam_copy(k, src, dst, o):
        to = cam_peer(o)
        return pltpu.make_async_remote_copy(
            src_ref=src(to[0]), dst_ref=dst, send_sem=cam_ss.at[k, o], recv_sem=cam_rs.at[k, o],
            device_id=to, device_id_type=MESH,
        )

    def wide_copy(k, src, dst, peer, o):
        to = peer(o)
        return pltpu.make_async_remote_copy(
            src_ref=src(to), dst_ref=dst, send_sem=wide_ss.at[k, o], recv_sem=wide_rs.at[k, o],
            device_id=to, device_id_type=MESH,
        )

    def w_copy(o):
        return cam_copy(0, lambda p: w_send.at[p], w_recv.at[cam], o)

    def pool_copy(o):
        return cam_copy(1, lambda p: pool_send, pool_recv.at[cam], o)

    def mix_copy(o):
        return cam_copy(2, lambda p: mix_send.at[p], mix_recv.at[cam], o)

    def gz_copy(o):
        return cam_copy(3, lambda p: gz_send, gz_recv.at[cam], o)

    def z_copy(o):
        return wide_copy(0, lambda to: z_send, z_recv.at[clip], clip_peer, o)

    def side_copy(o):
        return wide_copy(
            1, lambda to: side_send.at[lax.div(to[1] * SHARE, LANES)], side_recv.at[clip], clip_peer, o
        )

    def gu_copy(o):
        return wide_copy(2, lambda to: gu_send.at[to[0]], gu_recv.at[here], r_peer, o)

    def row_copy(step, o):
        return wide_copy(3 + step, lambda to: row_send.at[step], row_recv.at[step, here], r_peer, o)

    row8 = lax.broadcasted_iota(jnp.int32, (8, KEYS), 0)
    weights = jnp.zeros((8, KEYS), F32)
    for r in range(PAIR * PAIR):
        weights = jnp.where(row8 == r, jnp.sum(acc[r], axis=0, keepdims=True) * (1.0 / KEYS), weights)
    for p in range(N_CAM):
        w_send[p] = weights[:, p * TOK : (p + 1) * TOK]
    loop(1, N_CAM, lambda o: w_copy(o).start())
    w_recv[cam] = w_send[cam]
    loads[4].wait()
    loop(1, N_CAM, lambda o: w_copy(o).wait_recv())

    key_weight = w_recv[...].reshape(8 * N_CAM, TOK).astype(BF16)
    mix0 = dot(key_weight, xv[:TOK, :], NN)
    mix1 = dot(key_weight, xv[TOK:, :], NN)
    row64 = lax.broadcasted_iota(jnp.int32, (8 * N_CAM, D), 0)
    mixture = jnp.where(lax.rem(row64, 8) >= PAIR, mix1, mix0).astype(BF16)
    head_out = dot(mixture, wv[...], NN)
    lane8 = lax.broadcasted_iota(jnp.int32, (8, LANES), 1)
    sub8 = lax.broadcasted_iota(jnp.int32, (8, LANES), 0)
    own_head = lax.rem(sub8, PAIR) == lax.div(lane8, HD)
    for p in range(N_CAM):
        tile = head_out[p * 8 : (p + 1) * 8, p * LANES : (p + 1) * LANES]
        tile = jnp.where(own_head, tile, 0.0)
        pool_send[p : p + 1, :] = tile[0:1] + tile[1:2]
        pool_send[N_CAM + p : N_CAM + p + 1, :] = tile[2:3] + tile[3:4]
    loop(1, N_CAM, lambda o: pool_copy(o).start())
    pool_recv[cam] = pool_send[...]
    mixture_f = mixture.astype(F32)
    for p in range(N_CAM):
        mix_send[p] = mixture_f[p * 8 : p * 8 + PAIR * PAIR, :]
    loop(1, N_CAM, lambda o: mix_copy(o).start())
    mix_recv[cam] = mix_send[cam]
    loads[5].wait()
    loop(1, N_CAM, lambda o: pool_copy(o).wait_recv())
    pooled = jnp.sum(pool_recv[...], axis=0).astype(BF16)
    row16 = lax.broadcasted_iota(jnp.int32, (PAIR * N_CAM, LANES), 0)
    spread = jnp.concatenate(
        [jnp.where(lax.rem(row16, N_CAM) == p, pooled, jnp.zeros_like(pooled)) for p in range(N_CAM)], axis=1
    )
    z_rows = dot(spread, wp[...], NN)
    for b in range(PAIR):
        z_clip = jnp.sum(z_rows[b * N_CAM : (b + 1) * N_CAM], axis=0, keepdims=True)
        for j in range(2):
            z_send[2 * b + j : 2 * b + j + 1, :] = z_clip[:, j * LANES : (j + 1) * LANES]
    loop(1, N_CLIP, lambda o: z_copy(o).start())
    z_recv[clip] = z_send[...]

    loop(1, N_CAM, lambda o: mix_copy(o).wait_recv())
    mix_sum = jnp.sum(mix_recv[...], axis=0)
    pooled_f = pooled.astype(F32)
    for p in range(N_CAM):
        side_send[p, 0:1, :] = pooled_f[p : p + 1]
        side_send[p, 1:2, :] = pooled_f[N_CAM + p : N_CAM + p + 1]
        side_send[p, 2:6, :] = mix_sum[:, p * LANES : (p + 1) * LANES]
        side_send[p, 6:8, :] = jnp.zeros((2, LANES), F32)
    loop(1, N_Z, lambda o: proto_copy(o).wait_recv())
    loop(1, N_CLIP, lambda o: z_copy(o).wait_recv())
    loop(1, N_CLIP, lambda o: side_copy(o).start())
    side_recv[clip] = side_send[lax.div(clip * SHARE, LANES)]

    embed = jnp.concatenate(
        [jnp.concatenate([z_recv[:, 2 * b + j, :] for j in range(2)], axis=1) for b in range(PAIR)], axis=0
    )
    norm = jnp.sqrt(jnp.sum(embed * embed, axis=1, keepdims=True) + NORM_EPS)
    unit = embed / norm
    unit_buf[...] = unit
    norm_buf[...] = jnp.broadcast_to(norm, norm_buf.shape)
    unit_b = unit.astype(BF16)

    def total(step, sums):
        tall = jnp.broadcast_to(jnp.sum(sums, axis=1, keepdims=True), (LANES, LANES))
        row_send[step] = tall.T[:8, :]
        loop(1, N_R, lambda o: row_copy(step, o).start())
        row_recv[step, here] = row_send[step]
        loop(1, N_R, lambda o: row_copy(step, o).wait_recv())
        wide = jnp.sum(row_recv[step], axis=0)
        return jnp.broadcast_to(wide[0:1], (LANES, LANES)).T

    zero = jnp.zeros((CLIPS, LANES), F32)

    def first(s, carry):
        rows, probs = carry
        exps = jnp.exp(dot(unit_b, proto_all[s], NN) * (1.0 / SOFTMAX_TEMP))
        scores = exps * exps
        p_buf[s] = exps
        a_buf[s] = scores
        scaled = scores * (1.0 / jnp.sum(scores, axis=0, keepdims=True))
        return rows + fold(scaled), probs + fold(exps)

    rows, probs = lax.fori_loop(0, N_Z, first, (zero, zero))
    got = total(0, jnp.concatenate([rows, probs], axis=0))
    row_scale = 1.0 / got[:CLIPS]
    prob_scale = twice(1.0 / got[CLIPS:])
    for step in (1, 2):
        wide_scale = twice(row_scale)

        def again(s, rows):
            scores = a_buf[s]
            scale = 1.0 / jnp.sum(scores * wide_scale, axis=0, keepdims=True)
            v_buf[s] = jnp.broadcast_to(scale, (8, COLS))
            return rows + fold(scores * scale)

        rows = lax.fori_loop(0, N_Z, again, zero)
        row_scale = 1.0 / total(step, jnp.concatenate([rows, rows], axis=0))[:CLIPS]
    wide_scale = twice(row_scale)

    def assigned(s):
        return a_buf[s] * v_buf[s][0:1] * wide_scale

    def grads(s, carry):
        logit_grad = (PROTOS * (p_buf[s] * prob_scale - assigned(s))).astype(BF16)
        g_buf[s] = logit_grad
        return carry + dot(logit_grad, proto_all[s], NT)

    grad_unit = lax.fori_loop(0, N_Z, grads, jnp.zeros((CLIPS, BOT), F32))
    for p in range(N_CAM):
        gu_send[p] = grad_unit[p * 8 : (p + 1) * 8]
    loop(1, N_R, lambda o: gu_copy(o).start())
    gu_recv[here] = gu_send[cam]

    codes_out[...] = PROTOS * assigned(z)
    grad_proto = dot(unit_b, g_buf[z], TN)
    proto = pr[...].astype(F32)
    col_norm = jnp.sqrt(jnp.sum(proto * proto, axis=0, keepdims=True) + NORM_EPS)
    unit_proto = proto / col_norm
    proto_out[...] = (
        grad_proto - unit_proto * jnp.sum(unit_proto * grad_proto, axis=0, keepdims=True)
    ) / col_norm

    loop(1, N_R, lambda o: gu_copy(o).wait_recv())
    grad8 = jnp.sum(gu_recv[...], axis=0)
    mine = pl.ds(pl.multiple_of(cam * 8, 8), 8)
    unit8 = unit_buf[mine, :]
    grad8 = (grad8 - unit8 * jnp.sum(unit8 * grad8, axis=1, keepdims=True)) / norm_buf[mine, :]
    gz_send[...] = grad8.astype(BF16).astype(F32)
    loop(1, N_CAM, lambda o: gz_copy(o).start())
    gz_recv[cam] = gz_send[...]
    loop(1, N_CLIP, lambda o: side_copy(o).wait_recv())
    pooled_all = jnp.concatenate([side_recv[:, b, :] for b in range(PAIR)], axis=0).astype(BF16)
    loop(1, N_CAM, lambda o: gz_copy(o).wait_recv())
    grad_z = gz_recv[...].reshape(CLIPS, BOT).astype(BF16)

    part = pl.ds(pl.multiple_of(lax.rem(clip * SHARE, LANES), SHARE), SHARE)
    proj_tmp[...] = dot(pooled_all, grad_z, TN)
    proj_out[...] = proj_tmp[part, :]
    grad_pooled = dot(grad_z, wp[pl.ds(pl.multiple_of(cam * LANES, LANES), LANES), :], NT).astype(BF16)
    by_head = []
    for head in range(PAIR):
        mix_all = jnp.concatenate([side_recv[:, 2 + PAIR * b + head, :] for b in range(PAIR)], axis=0)
        high = mix_all.astype(BF16)
        low = (mix_all - high.astype(F32)).astype(BF16)
        by_head.append(dot(high, grad_pooled, TN) + dot(low, grad_pooled, TN))
    lane = lax.broadcasted_iota(jnp.int32, (LANES, LANES), 1)
    value_tmp[...] = jnp.where(lane < HD, by_head[0], by_head[1])
    value_out[...] = value_tmp[part, :]

    for b in range(PAIR):
        loop(1, N_CAM, lambda o: qk_copy(b, o).wait_send())
    loop(1, N_Z, lambda o: proto_copy(o).wait_send())
    for copy in (w_copy, pool_copy, mix_copy, gz_copy):
        loop(1, N_CAM, lambda o: copy(o).wait_send())
    for copy in (z_copy, side_copy):
        loop(1, N_CLIP, lambda o: copy(o).wait_send())
    loop(1, N_R, lambda o: gu_copy(o).wait_send())
    for step in range(3):
        loop(1, N_R, lambda o: row_copy(step, o).wait_send())


def local(tokens, w_query, w_key, w_value, w_proj, prototypes):
    vmem, dma = pltpu.VMEM, pltpu.SemaphoreType.DMA
    codes, proto_grad, proj_grad, value_grad = pl.pallas_call(
        kernel,
        out_shape=(
            jax.ShapeDtypeStruct((CLIPS, COLS), F32),
            jax.ShapeDtypeStruct((BOT, COLS), F32),
            jax.ShapeDtypeStruct((SHARE, BOT), F32),
            jax.ShapeDtypeStruct((SHARE, LANES), F32),
        ),
        in_specs=[pl.BlockSpec(memory_space=pl.ANY)] * 6,
        out_specs=[pl.BlockSpec(memory_space=pltpu.VMEM)] * 4,
        scratch_shapes=[
            vmem((PAIR * TOK, D), BF16), vmem((D, D), BF16), vmem((D, D), BF16), vmem((D, D), BF16),
            vmem((D, BOT), BF16), vmem((BOT, COLS), BF16),
            vmem((N_Z, BOT, COLS), BF16),
            vmem((PAIR, N_CAM, 2, TOK, LANES), BF16), vmem((PAIR, N_CAM, 2, TOK, LANES), BF16),
            vmem((PAIR * PAIR, 8, KEYS), F32),
            vmem((N_CAM, 8, TOK), F32), vmem((N_CAM, 8, TOK), F32),
            vmem((N_CAM, PAIR * PAIR, D), F32), vmem((N_CAM, PAIR * PAIR, D), F32),
            vmem((PAIR * N_CAM, LANES), F32), vmem((N_CAM, PAIR * N_CAM, LANES), F32),
            vmem((4, LANES), F32), vmem((N_CLIP, 4, LANES), F32),
            vmem((N_CAM, 8, LANES), F32), vmem((N_CLIP, 8, LANES), F32),
            vmem((N_Z, CLIPS, COLS), F32), vmem((N_Z, CLIPS, COLS), F32), vmem((N_Z, 8, COLS), F32),
            vmem((N_Z, CLIPS, COLS), BF16), vmem((CLIPS, BOT), F32), vmem((CLIPS, BOT), F32),
            vmem((3, 8, LANES), F32), vmem((3, N_R, 8, LANES), F32),
            vmem((N_CAM, 8, BOT), F32), vmem((N_R, 8, BOT), F32),
            vmem((8, BOT), F32), vmem((N_CAM, 8, BOT), F32),
            vmem((LANES, BOT), F32), vmem((LANES, LANES), F32),
            dma((6,)), dma((PAIR,)), dma((PAIR, N_CAM)), dma((PAIR, N_CAM)), dma((4, N_CAM)), dma((4, N_CAM)),
            dma((N_Z,)), dma((N_Z,)), dma((6, N_CLIP)), dma((6, N_CLIP)),
        ],
        compiler_params=pltpu.CompilerParams(
            collective_id=0, has_side_effects=True, vmem_limit_bytes=58 * 2**20
        ),
    )(tokens.reshape(PAIR * TOK, D), w_query, w_key, w_value, w_proj, prototypes)
    codes = codes.reshape(PAIR, N_CLIP, COLS).transpose(1, 0, 2).reshape(CLIPS, COLS)
    return codes, proto_grad, proj_grad, value_grad


def solution(mesh):
    assert mesh.shape["cam"] == N_CAM and mesh.shape["clip"] == N_CLIP
    in_specs = (P("clip", "cam", None, None), P(), P(), P(), P(), P(None, ("cam", "clip")))
    out_specs = (
        P(None, ("cam", "clip")),
        P(None, ("cam", "clip")),
        P("clip", None),
        P("clip", "cam"),
    )
    return jax.shard_map(local, mesh=mesh, in_specs=in_specs, out_specs=out_specs, check_vma=False)
```

time: 1160 us -> 103 us (0.09)
  waiting for transfers between devices: 680 us -> 0 us
  blocking collectives: 296 us -> 0 us
  matrix products: 107 us -> 0 us
  Pallas kernels: 0 us -> 96.3 us
  local copies, waits for them, and re-layouts: 54.6 us -> 5.93 us
  between operations: 14.9 us -> 0.64 us
    reduce_scatter x4 -> x0, waiting for transfers between devices: 498 us -> none  [the longest x1 218 us: local(): lax.psum_scatter(jnp.einsum('cd,ce->de', piece, grad_embed_b, preferred_e...]
    psum x5 -> x0, blocking collectives: 262 us -> none  [the longest x3 231 us: local(): row_total = lax.psum(jnp.sum(assign, axis=1), ('cam', 'clip'))]
    unnamed x7 -> x0, waiting for transfers between devices: 133 us -> none
    pallas_call x0 -> x1, Pallas kernels: none -> 96.3 us  [local(): pl.pallas_call(kernel, out_shape=(jax.ShapeDtypeStruct((CLIPS, COLS), F32...]
    dot_general x19 -> x0, matrix products: 57.4 us -> none  [the longest x8 38.4 us: column_sums(): jnp.einsum('ihe,jhe->hij', query_rows, key_rows, preferred_element_type=j...]
    div x8 -> x0, matrix products: 49.5 us -> none  [column_sums(): probs = exponent_values / jnp.sum(exponent_values, axis=2, keepdims=True)]
    all_gather x1 -> x0, waiting for transfers between devices: 48.7 us -> none  [local(): lax.all_gather(key_rows.reshape(clips, 1, TOK, D), 'cam', axis=1, tiled=T...]
    all_gather x1 -> x0, blocking collectives: 33.8 us -> none  [local(): all_units = lax.all_gather(unit_b, 'clip', axis=0, tiled=True)]
  transfers between devices with their start and end apart: 6 -> 0, of which waited for: 6 -> 0; matrix products, arithmetic and copies ran while one was open for 1% -> 0% of each run, Pallas kernels for 0% -> 0%
where the time goes in v1:
time: 103 us
  Pallas kernels  96.3 us (93%)
  local copies, waits for them, and re-layouts  5.93 us (6%)
    pallas_call x1, Pallas kernels, local(): pl.pallas_call(kernel, out_shape=(jax.ShapeDtypeStruct((CLIPS, COLS), F32...  96.3 us
    unnamed x3, local copies, waits for them, and re-layouts  4.36 us

profile of v1, /device:TPU:1, one launch (start us, length us, event | category | flops | bytes accessed | tf_op | source)
XLA Modules:
  0.0 102.9 jit_solution(15176587898135856761)
XLA Ops:
  0.6 96.3 %shard_map.93 = (f32[64,256]{1,0:T(8,128)}, f32[256,256]{1,0:T(8,128)}, f32[32,256]{1,0:T(8,128)}, f32[32,128]{1,0:T(8,128)}) custom-call(bf16[512,1024]{1,0:T(8,128)(2,1)} %bitcast.4, bf16[1024,1024]{1,0:T(8,128)(2,1)} %wq_in.1, bf16[1024,1024]{1,0:T(8,128)(2,1)} %wk_in.1, bf16[1024,1024]{1,0:T(8,128)(2,1)} %wv_in.1, bf16[1024,256]{1,0:T(8,128)(2,1)} %wp_in.1, ...), custom_call_target="tpu_custom_call" | custom-call | tf_op jit(solution)/shard_map/pallas_call | solution.py:392
  96.9 0.9 copy.10
  97.8 0.7 reshape.19
  98.5 1.7 %copy.14 = f32[256,256]{1,0:T(8,128)} copy(f32[256,256]{1,0:T(8,128)} %get-tuple-element.17) | data formatting | bytes 524288
  100.2 1.4 %copy.15 = f32[32,256]{1,0:T(8,128)} copy(f32[32,256]{1,0:T(8,128)} %get-tuple-element.18) | data formatting | bytes 65536
  101.5 1.3 %copy.16 = f32[32,128]{1,0:T(8,128)} copy(f32[32,128]{1,0:T(8,128)} %get-tuple-element.19) | data formatting | bytes 32768

commit v2 on v1

v2 whole, which is shorter than its diff:
```python
import functools

import jax
import jax.numpy as jnp
from jax import lax
from jax.experimental import pallas as pl
from jax.experimental.pallas import tpu as pltpu
from jax.sharding import PartitionSpec as P

D = 1024
HD = 64
H = 16
BOT = 256
PROTOS = 65536
TOK = 256
CLIPS = 64
N_CAM = 8
N_CLIP = 32
N_Z = 8
N_Y = N_CLIP // N_Z
N_R = N_CAM * N_Y
PAIR = 2
LANES = 128
COLS = PROTOS // (N_CAM * N_CLIP)
SHARE = D // N_CLIP
KEYS = N_CAM * TOK
PIECES = 4
PIECE = TOK // PIECES
ROWS = N_CAM * PIECE

SINK_EPS = 0.05
SOFTMAX_TEMP = 0.1
NORM_EPS = 1e-06
LOG2_E = 1.4426950408889634

MESH = pl.DeviceIdType.MESH
F32 = jnp.float32
BF16 = jnp.bfloat16


CAM_ORDER = (4, 3, 5, 2, 6, 7, 1)
Y_ORDER = (2, 1, 3, 0)
Z_ORDER = (4, 3, 5, 2, 6, 1, 7, 0)
CLIP_ORDER = tuple((oy, oz) for oy in Y_ORDER for oz in Z_ORDER if (oy, oz) != (0, 0))
R_ORDER = tuple((oy, oc) for oy in Y_ORDER for oc in CAM_ORDER + (0,) if (oy, oc) != (0, 0))


def dot(a, b, dims):
    return lax.dot_general(a, b, (dims, ((), ())), preferred_element_type=F32)


NN = ((1,), (0,))
NT = ((1,), (1,))
TN = ((0,), (0,))


def fold(a):
    return a[:, :LANES] + a[:, LANES:]


def twice(a):
    return jnp.concatenate([a, a], axis=1)


def kernel(
    x_in, wq_in, wk_in, wv_in, wp_in, pr_in,
    codes_out, proto_out, proj_out, value_out,
    xv, wq, wk, wv, wp, pr,
    proto_all, k_send, k_recv, q_send, q_recv, acc,
    w_send, w_recv, mix_send, mix_recv, pool_send, pool_recv,
    z_send, z_recv, side_send, side_recv,
    a_buf, p_buf, v_buf, g_buf, unit_buf, norm_buf,
    row_send, row_recv, gu_send, gu_recv, gz_send, gz_recv,
    proj_tmp, value_tmp,
    load_sem, own_sem, y_sem, qk_ss, qk_rs, cam_ss, cam_rs, proto_ss, proto_rs, wide_ss, wide_rs,
):
    cam = lax.axis_index("cam")
    clip = lax.axis_index("clip")
    y, z = lax.div(clip, N_Z), lax.rem(clip, N_Z)
    here = y * N_CAM + cam

    def cam_peer(o):
        return (lax.rem(cam + o, N_CAM), clip)

    def yz_peer(oy, oz):
        return (cam, lax.rem(y + oy, N_Y) * N_Z + lax.rem(z + oz, N_Z))

    def r_peer(oy, oc):
        return (lax.rem(cam + oc, N_CAM), lax.rem(y + oy, N_Y) * N_Z + z)

    def loop(lo, hi, step):
        def body(i, carry):
            step(i)
            return carry

        lax.fori_loop(lo, hi, body, 0)

    barrier = pltpu.get_barrier_semaphore()
    for oz in Z_ORDER[:-1]:
        pl.semaphore_signal(barrier, inc=1, device_id=yz_peer(0, oz), device_id_type=MESH)
    for oy in Y_ORDER[:-1]:
        pl.semaphore_signal(barrier, inc=1, device_id=yz_peer(oy, 0), device_id_type=MESH)
    for o in CAM_ORDER:
        pl.semaphore_signal(barrier, inc=1, device_id=cam_peer(o), device_id_type=MESH)

    loads = [
        pltpu.make_async_copy(x_in.at[pl.ds(0, TOK)], xv.at[pl.ds(0, TOK)], load_sem.at[0]),
        pltpu.make_async_copy(wk_in, wk, load_sem.at[1]),
        pltpu.make_async_copy(wq_in, wq, load_sem.at[2]),
        pltpu.make_async_copy(x_in.at[pl.ds(TOK, TOK)], xv.at[pl.ds(TOK, TOK)], load_sem.at[3]),
        pltpu.make_async_copy(pr_in, pr, load_sem.at[4]),
        pltpu.make_async_copy(wv_in, wv, load_sem.at[5]),
        pltpu.make_async_copy(wp_in, wp, load_sem.at[6]),
    ]
    for load in loads:
        load.start()

    def project_keys(b):
        rows = xv[b * TOK : (b + 1) * TOK, :]
        for j in range(D // 256):
            got = dot(rows, wk[:, j * 256 : (j + 1) * 256], NN).astype(BF16)
            k_send[b, 2 * j] = got[:, :LANES]
            k_send[b, 2 * j + 1] = got[:, LANES:]

    def project_queries(b):
        rows = xv[b * TOK : (b + 1) * TOK, :]
        for j in range(D // 256):
            got = dot(rows, wq[:, j * 256 : (j + 1) * 256], NN).astype(BF16)
            q_send[b, 2 * j] = got[:, :LANES].reshape(PIECES, PIECE, LANES)
            q_send[b, 2 * j + 1] = got[:, LANES:].reshape(PIECES, PIECE, LANES)

    def remote(src, dst, send_sem, recv_sem, to):
        return pltpu.make_async_remote_copy(
            src_ref=src, dst_ref=dst, send_sem=send_sem, recv_sem=recv_sem,
            device_id=to, device_id_type=MESH,
        )

    def k_copy(b, o):
        to = cam_peer(o)
        return remote(k_send.at[b, to[0]], k_recv.at[b, cam], qk_ss.at[b, PIECES, o], qk_rs.at[b, PIECES, o], to)

    def q_copy(b, part, o):
        to = cam_peer(o)
        return remote(
            q_send.at[b, to[0], part], q_recv.at[b, part, cam], qk_ss.at[b, part, o], qk_rs.at[b, part, o], to
        )

    def own_k(b):
        return pltpu.make_async_copy(k_send.at[b, cam], k_recv.at[b, cam], own_sem.at[b, PIECES])

    def own_q(b, part):
        return pltpu.make_async_copy(q_send.at[b, cam, part], q_recv.at[b, part, cam], own_sem.at[b, part])

    def send_keys(b):
        for o in CAM_ORDER:
            k_copy(b, o).start()
        own_k(b).start()

    def send_queries(b):
        for part in range(PIECES):
            for o in CAM_ORDER:
                q_copy(b, part, o).start()
            own_q(b, part).start()

    def proto_copy(i):
        return remote(proto_all.at[z], proto_all.at[z], proto_ss.at[i], proto_rs.at[i], yz_peer(0, Z_ORDER[i]))

    loads[0].wait()
    loads[1].wait()
    project_keys(0)
    pl.semaphore_wait(barrier, N_CAM - 1 + N_Y - 1 + N_Z - 1)
    send_keys(0)
    for oy in Y_ORDER[:-1]:
        pl.semaphore_signal(y_sem, inc=1, device_id=yz_peer(oy, 0), device_id_type=MESH)
    loads[2].wait()
    project_queries(0)
    send_queries(0)
    loads[3].wait()
    project_keys(1)
    send_keys(1)
    project_queries(1)
    send_queries(1)

    loads[4].wait()
    proto = pr[...].astype(F32)
    col_norm = jnp.sqrt(jnp.sum(proto * proto, axis=0, keepdims=True) + NORM_EPS)
    proto_all[z] = (proto / col_norm).astype(BF16)
    for i in range(N_Z - 1):
        proto_copy(i).start()

    acc[...] = jnp.zeros_like(acc)
    lane_q = lax.broadcasted_iota(jnp.int32, (ROWS, LANES), 1)

    def attend(b):
        loop(1, N_CAM, lambda o: k_copy(b, o).wait_recv())
        own_k(b).wait()

        def piece(part):
            loop(1, N_CAM, lambda o: q_copy(b, part, o).wait_recv())
            own_q(b, part).wait()
            keys = k_recv[b].reshape(KEYS, LANES)
            both = q_recv[b, part].reshape(ROWS, LANES)
            for head in range(PAIR):
                rows = jnp.where((lane_q < HD) == (head == 0), both, jnp.zeros_like(both))
                weights = jnp.exp2(dot(rows, keys, NT) * (HD ** (-0.5) * LOG2_E))
                weights = weights * (1.0 / jnp.sum(weights, axis=1, keepdims=True))
                acc[b * PAIR + head] += jnp.sum(weights.reshape(ROWS // 8, 8, KEYS), axis=0)

        loop(0, PIECES, piece)

    loop(0, PAIR, attend)

    class Exchange:
        def __init__(self, order, peer, src, dst, send_sem, recv_sem):
            self.order, self.peer, self.src, self.dst = order, peer, src, dst
            self.send_sem, self.recv_sem = send_sem, recv_sem

        def copy(self, i, to):
            return remote(self.src(to), self.dst, self.send_sem(i), self.recv_sem(i), to)

        def start(self):
            for i, o in enumerate(self.order):
                self.copy(i, self.peer(o)).start()

        def landed(self):
            to = self.peer(self.order[0])
            loop(0, len(self.order), lambda i: self.copy(i, to).wait_recv())

        def left(self):
            to = self.peer(self.order[0])
            loop(0, len(self.order), lambda i: self.copy(i, to).wait_send())

    def cam_exchange(k, src, dst):
        return Exchange(CAM_ORDER, cam_peer, src, dst, lambda i: cam_ss.at[k, i], lambda i: cam_rs.at[k, i])

    def wide_exchange(k, order, peer, src, dst):
        return Exchange(
            order, lambda o: peer(*o), src, dst, lambda i: wide_ss.at[k, i], lambda i: wide_rs.at[k, i]
        )

    w_out = cam_exchange(0, lambda to: w_send.at[to[0]], w_recv.at[cam])
    pool_out = cam_exchange(1, lambda to: pool_send, pool_recv.at[cam])
    mix_out = cam_exchange(2, lambda to: mix_send.at[to[0]], mix_recv.at[cam])
    gz_out = cam_exchange(3, lambda to: gz_send, gz_recv.at[cam])
    z_out = wide_exchange(0, CLIP_ORDER, yz_peer, lambda to: z_send, z_recv.at[clip])
    side_out = wide_exchange(
        1, CLIP_ORDER, yz_peer, lambda to: side_send.at[lax.div(to[1] * SHARE, LANES)], side_recv.at[clip]
    )
    gu_out = wide_exchange(2, R_ORDER, r_peer, lambda to: gu_send.at[to[0]], gu_recv.at[here])

    def row_exchange(step):
        return wide_exchange(3 + step, R_ORDER, r_peer, lambda to: row_send.at[step], row_recv.at[step, here])

    row_out = [row_exchange(step) for step in range(3)]

    row8 = lax.broadcasted_iota(jnp.int32, (8, KEYS), 0)
    weights = jnp.zeros((8, KEYS), F32)
    for r in range(PAIR * PAIR):
        weights = jnp.where(row8 == r, jnp.sum(acc[r], axis=0, keepdims=True) * (1.0 / KEYS), weights)
    for p in range(N_CAM):
        w_send[p] = weights[:, p * TOK : (p + 1) * TOK]
    w_out.start()
    w_recv[cam] = w_send[cam]
    loads[5].wait()
    w_out.landed()

    key_weight = w_recv[...].reshape(8 * N_CAM, TOK).astype(BF16)
    mix0 = dot(key_weight, xv[:TOK, :], NN)
    mix1 = dot(key_weight, xv[TOK:, :], NN)
    row64 = lax.broadcasted_iota(jnp.int32, (8 * N_CAM, D), 0)
    mixture = jnp.where(lax.rem(row64, 8) >= PAIR, mix1, mix0).astype(BF16)
    head_out = dot(mixture, wv[...], NN)
    lane8 = lax.broadcasted_iota(jnp.int32, (8, LANES), 1)
    sub8 = lax.broadcasted_iota(jnp.int32, (8, LANES), 0)
    own_head = lax.rem(sub8, PAIR) == lax.div(lane8, HD)
    for p in range(N_CAM):
        tile = head_out[p * 8 : (p + 1) * 8, p * LANES : (p + 1) * LANES]
        tile = jnp.where(own_head, tile, 0.0)
        pool_send[p : p + 1, :] = tile[0:1] + tile[1:2]
        pool_send[N_CAM + p : N_CAM + p + 1, :] = tile[2:3] + tile[3:4]
    pool_out.start()
    pool_recv[cam] = pool_send[...]
    mixture_f = mixture.astype(F32)
    for p in range(N_CAM):
        mix_send[p] = mixture_f[p * 8 : p * 8 + PAIR * PAIR, :]
    mix_out.start()
    mix_recv[cam] = mix_send[cam]
    loads[6].wait()
    pool_out.landed()
    pooled = jnp.sum(pool_recv[...], axis=0).astype(BF16)
    row16 = lax.broadcasted_iota(jnp.int32, (PAIR * N_CAM, LANES), 0)
    spread = jnp.concatenate(
        [jnp.where(lax.rem(row16, N_CAM) == p, pooled, jnp.zeros_like(pooled)) for p in range(N_CAM)], axis=1
    )
    z_rows = dot(spread, wp[...], NN)
    for b in range(PAIR):
        z_clip = jnp.sum(z_rows[b * N_CAM : (b + 1) * N_CAM], axis=0, keepdims=True)
        for j in range(2):
            z_send[2 * b + j : 2 * b + j + 1, :] = z_clip[:, j * LANES : (j + 1) * LANES]
    pl.semaphore_wait(y_sem, N_Y - 1)
    z_out.start()
    z_recv[clip] = z_send[...]

    mix_out.landed()
    mix_sum = jnp.sum(mix_recv[...], axis=0)
    pooled_f = pooled.astype(F32)
    for p in range(N_CAM):
        side_send[p, 0:1, :] = pooled_f[p : p + 1]
        side_send[p, 1:2, :] = pooled_f[N_CAM + p : N_CAM + p + 1]
        side_send[p, 2:6, :] = mix_sum[:, p * LANES : (p + 1) * LANES]
        side_send[p, 6:8, :] = jnp.zeros((2, LANES), F32)
    for i in range(N_Z - 1):
        proto_copy(i).wait_recv()
    z_out.landed()
    side_out.start()
    side_recv[clip] = side_send[lax.div(clip * SHARE, LANES)]

    embed = jnp.concatenate(
        [jnp.concatenate([z_recv[:, 2 * b + j, :] for j in range(2)], axis=1) for b in range(PAIR)], axis=0
    )
    norm = jnp.sqrt(jnp.sum(embed * embed, axis=1, keepdims=True) + NORM_EPS)
    unit = embed / norm
    unit_buf[...] = unit
    norm_buf[...] = jnp.broadcast_to(norm, norm_buf.shape)
    unit_b = unit.astype(BF16)

    def total(step, sums):
        tall = jnp.broadcast_to(jnp.sum(sums, axis=1, keepdims=True), (LANES, LANES))
        row_send[step] = tall.T[:1, :]
        row_out[step].start()
        row_recv[step, here] = row_send[step]
        row_out[step].landed()
        wide = jnp.sum(row_recv[step], axis=0)
        return jnp.broadcast_to(wide, (LANES, LANES)).T

    zero = jnp.zeros((CLIPS, LANES), F32)

    def first(s, carry):
        rows, probs = carry
        exps = jnp.exp(dot(unit_b, proto_all[s], NN) * (1.0 / SOFTMAX_TEMP))
        scores = exps * exps
        p_buf[s] = exps
        a_buf[s] = scores
        scaled = scores * (1.0 / jnp.sum(scores, axis=0, keepdims=True))
        return rows + fold(scaled), probs + fold(exps)

    rows, probs = lax.fori_loop(0, N_Z, first, (zero, zero))
    got = total(0, jnp.concatenate([rows, probs], axis=0))
    row_scale = 1.0 / got[:CLIPS]
    prob_scale = twice(1.0 / got[CLIPS:])
    for step in (1, 2):
        wide_scale = twice(row_scale)

        def again(s, rows):
            scores = a_buf[s]
            scale = 1.0 / jnp.sum(scores * wide_scale, axis=0, keepdims=True)
            v_buf[s] = jnp.broadcast_to(scale, (8, COLS))
            return rows + fold(scores * scale)

        rows = lax.fori_loop(0, N_Z, again, zero)
        row_scale = 1.0 / total(step, jnp.concatenate([rows, rows], axis=0))[:CLIPS]
    wide_scale = twice(row_scale)

    def assigned(s):
        return a_buf[s] * v_buf[s][0:1] * wide_scale

    def grads(s, carry):
        logit_grad = (PROTOS * (p_buf[s] * prob_scale - assigned(s))).astype(BF16)
        g_buf[s] = logit_grad
        return carry + dot(logit_grad, proto_all[s], NT)

    grad_unit = lax.fori_loop(0, N_Z, grads, jnp.zeros((CLIPS, BOT), F32))
    for p in range(N_CAM):
        gu_send[p] = grad_unit[p * 8 : (p + 1) * 8]
    gu_out.start()
    gu_recv[here] = gu_send[cam]

    codes_out[...] = PROTOS * assigned(z)
    grad_proto = dot(unit_b, g_buf[z], TN)
    proto = pr[...].astype(F32)
    col_norm = jnp.sqrt(jnp.sum(proto * proto, axis=0, keepdims=True) + NORM_EPS)
    unit_proto = proto / col_norm
    proto_out[...] = (
        grad_proto - unit_proto * jnp.sum(unit_proto * grad_proto, axis=0, keepdims=True)
    ) / col_norm

    gu_out.landed()
    grad8 = jnp.sum(gu_recv[...], axis=0)
    mine = pl.ds(pl.multiple_of(cam * 8, 8), 8)
    unit8 = unit_buf[mine, :]
    grad8 = (grad8 - unit8 * jnp.sum(unit8 * grad8, axis=1, keepdims=True)) / norm_buf[mine, :]
    gz_send[...] = grad8.astype(BF16).astype(F32)
    gz_out.start()
    gz_recv[cam] = gz_send[...]
    side_out.landed()
    pooled_all = jnp.concatenate([side_recv[:, b, :] for b in range(PAIR)], axis=0).astype(BF16)
    gz_out.landed()
    grad_z = gz_recv[...].reshape(CLIPS, BOT).astype(BF16)

    part = pl.ds(pl.multiple_of(lax.rem(clip * SHARE, LANES), SHARE), SHARE)
    proj_tmp[...] = dot(pooled_all, grad_z, TN)
    proj_out[...] = proj_tmp[part, :]
    grad_pooled = dot(grad_z, wp[pl.ds(pl.multiple_of(cam * LANES, LANES), LANES), :], NT).astype(BF16)
    by_head = []
    for head in range(PAIR):
        mix_all = jnp.concatenate([side_recv[:, 2 + PAIR * b + head, :] for b in range(PAIR)], axis=0)
        high = mix_all.astype(BF16)
        low = (mix_all - high.astype(F32)).astype(BF16)
        by_head.append(dot(high, grad_pooled, TN) + dot(low, grad_pooled, TN))
    lane = lax.broadcasted_iota(jnp.int32, (LANES, LANES), 1)
    value_tmp[...] = jnp.where(lane < HD, by_head[0], by_head[1])
    value_out[...] = value_tmp[part, :]

    def left(b):
        loop(1, N_CAM, lambda o: k_copy(b, o).wait_send())
        loop(0, PIECES, lambda part: loop(1, N_CAM, lambda o: q_copy(b, part, o).wait_send()))

    loop(0, PAIR, left)
    for i in range(N_Z - 1):
        proto_copy(i).wait_send()
    for out in [w_out, pool_out, mix_out, gz_out, z_out, side_out, gu_out] + row_out:
        out.left()


def finish(codes, proto_grad, proj_grad, value_grad, codes_out, proto_out, proj_out, value_out, order):
    for j in range(COLS // LANES):
        columns = slice(j * LANES, (j + 1) * LANES)
        for b in range(PAIR):
            order[j, pl.ds(b, N_CLIP, stride=PAIR), :] = codes[b * N_CLIP : (b + 1) * N_CLIP, columns]
        codes_out[:, columns] = order[j]
    proto_out[...] = proto_grad[...]
    proj_out[...] = proj_grad[...]
    value_out[...] = value_grad[...]


def local(tokens, w_query, w_key, w_value, w_proj, prototypes):
    vmem, dma = pltpu.VMEM, pltpu.SemaphoreType.DMA
    shapes = (
        jax.ShapeDtypeStruct((CLIPS, COLS), F32),
        jax.ShapeDtypeStruct((BOT, COLS), F32),
        jax.ShapeDtypeStruct((SHARE, BOT), F32),
        jax.ShapeDtypeStruct((SHARE, LANES), F32),
    )
    got = pl.pallas_call(
        kernel,
        out_shape=shapes,
        in_specs=[pl.BlockSpec(memory_space=pl.ANY)] * 6,
        out_specs=[pl.BlockSpec(memory_space=pltpu.VMEM)] * 4,
        scratch_shapes=[
            vmem((PAIR * TOK, D), BF16), vmem((D, D), BF16), vmem((D, D), BF16), vmem((D, D), BF16),
            vmem((D, BOT), BF16), vmem((BOT, COLS), BF16),
            vmem((N_Z, BOT, COLS), BF16),
            vmem((PAIR, N_CAM, TOK, LANES), BF16), vmem((PAIR, N_CAM, TOK, LANES), BF16),
            vmem((PAIR, N_CAM, PIECES, PIECE, LANES), BF16), vmem((PAIR, PIECES, N_CAM, PIECE, LANES), BF16),
            vmem((PAIR * PAIR, 8, KEYS), F32),
            vmem((N_CAM, 8, TOK), F32), vmem((N_CAM, 8, TOK), F32),
            vmem((N_CAM, PAIR * PAIR, D), F32), vmem((N_CAM, PAIR * PAIR, D), F32),
            vmem((PAIR * N_CAM, LANES), F32), vmem((N_CAM, PAIR * N_CAM, LANES), F32),
            vmem((4, LANES), F32), vmem((N_CLIP, 4, LANES), F32),
            vmem((N_CAM, 8, LANES), F32), vmem((N_CLIP, 8, LANES), F32),
            vmem((N_Z, CLIPS, COLS), F32), vmem((N_Z, CLIPS, COLS), F32), vmem((N_Z, 8, COLS), F32),
            vmem((N_Z, CLIPS, COLS), BF16), vmem((CLIPS, BOT), F32), vmem((CLIPS, BOT), F32),
            vmem((3, 1, LANES), F32), vmem((3, N_R, 1, LANES), F32),
            vmem((N_CAM, 8, BOT), F32), vmem((N_R, 8, BOT), F32),
            vmem((8, BOT), F32), vmem((N_CAM, 8, BOT), F32),
            vmem((LANES, BOT), F32), vmem((LANES, LANES), F32),
            dma((7,)), dma((PAIR, PIECES + 1)), pltpu.SemaphoreType.REGULAR,
            dma((PAIR, PIECES + 1, N_CAM)), dma((PAIR, PIECES + 1, N_CAM)), dma((4, N_CAM)), dma((4, N_CAM)),
            dma((N_Z,)), dma((N_Z,)), dma((6, N_CLIP)), dma((6, N_CLIP)),
        ],
        compiler_params=pltpu.CompilerParams(
            collective_id=0, has_side_effects=True, vmem_limit_bytes=58 * 2**20
        ),
    )(tokens.reshape(PAIR * TOK, D), w_query, w_key, w_value, w_proj, prototypes)
    return pl.pallas_call(
        finish,
        out_shape=shapes,
        in_specs=[pl.BlockSpec(memory_space=pltpu.VMEM)] * 4,
        out_specs=[pl.BlockSpec(memory_space=pltpu.VMEM)] * 4,
        scratch_shapes=[vmem((COLS // LANES, CLIPS, LANES), F32)],
    )(*got)


def solution(mesh):
    assert mesh.shape["cam"] == N_CAM and mesh.shape["clip"] == N_CLIP
    in_specs = (P("clip", "cam", None, None), P(), P(), P(), P(), P(None, ("cam", "clip")))
    out_specs = (
        P(None, ("cam", "clip")),
        P(None, ("cam", "clip")),
        P("clip", None),
        P("clip", "cam"),
    )
    return jax.shard_map(local, mesh=mesh, in_specs=in_specs, out_specs=out_specs, check_vma=False)
```

time: 103 us -> 93.6 us (0.909)
  local copies, waits for them, and re-layouts: 5.93 us -> 0 us
  Pallas kernels: 96.3 us -> 92.9 us
    unnamed x3 -> x0, local copies, waits for them, and re-layouts: 4.36 us -> none
    pallas_call x1 -> x2, Pallas kernels: 96.3 us -> 92.9 us  [the longest x1 91.2 us: local(): pl.pallas_call(kernel, out_shape=shapes, in_specs=[pl.BlockSpec(memory_sp...]
where the time goes in v2:
time: 93.6 us; the launch traced here: 93.5 us
  Pallas kernels  92.9 us (99%)
    pallas_call x1, Pallas kernels, local(): pl.pallas_call(kernel, out_shape=shapes, in_specs=[pl.BlockSpec(memory_sp...  91.2 us

profile of v2, /device:TPU:1, one launch (start us, length us, event | category | flops | bytes accessed | tf_op | source)
XLA Modules:
  0.0 93.5 jit_solution(13365318972926065764)
XLA Ops:
  0.6 91.2 %shard_map.93 = (f32[64,256]{1,0:T(8,128)}, f32[256,256]{1,0:T(8,128)}, f32[32,256]{1,0:T(8,128)}, f32[32,128]{1,0:T(8,128)}) custom-call(bf16[512,1024]{1,0:T(8,128)(2,1)} %bitcast.1, bf16[1024,1024]{1,0:T(8,128)(2,1)} %wq_in.1, bf16[1024,1024]{1,0:T(8,128)(2,1)} %wk_in.1, bf16[1024,1024]{1,0:T(8,128)(2,1)} %wv_in.1, bf16[1024,256]{1,0:T(8,128)(2,1)} %wp_in.1, ...), custom_call_target="tpu_custom_call" | custom-call | tf_op jit(solution)/shard_map/pallas_call | solution.py:444
  91.8 1.7 %shard_map.94 = (f32[64,256]{1,0:T(8,128)}, f32[256,256]{1,0:T(8,128)}, f32[32,256]{1,0:T(8,128)}, f32[32,128]{1,0:T(8,128)}) custom-call(f32[64,256]{1,0:T(8,128)} %get-tuple-element.8.codes, f32[256,256]{1,0:T(8,128)} %get-tuple-element.9.proto_grad, f32[32,256]{1,0:T(8,128)} %get-tuple-element.10.proj_grad, f32[32,128]{1,0:T(8,128)} %get-tuple-element.11.value_grad), custom_call_target="tpu_custom_call" | custom-call | tf_op jit(solution)/shard_map/pallas_call | solution.py:475

commit v3 on v2

--- a/solution.py
+++ b/solution.py
@@ -54,6 +54,13 @@
 TN = ((0,), (0,))
 
 
+def split_dot(a, b):
+    high = a.astype(BF16)
+    low = (a - high.astype(F32)).astype(BF16)
+    got = dot(jnp.concatenate([high, low], axis=0), b, NT)
+    return got[: a.shape[0]] + got[a.shape[0] :]
+
+
 def fold(a):
     return a[:, :LANES] + a[:, LANES:]
 
@@ -69,8 +76,8 @@
     proto_all, k_send, k_recv, q_send, q_recv, acc,
     w_send, w_recv, mix_send, mix_recv, pool_send, pool_recv,
     z_send, z_recv, side_send, side_recv,
-    a_buf, p_buf, v_buf, g_buf, unit_buf, norm_buf,
-    row_send, row_recv, gu_send, gu_recv, gz_send, gz_recv,
+    a_buf, p_buf, unit_buf, norm_buf, prob_buf, scale_buf,
+    row_send, row_recv, gs_send, gs_recv, gu_send, gu_recv, gz_send, gz_recv,
     proj_tmp, value_tmp,
     load_sem, own_sem, y_sem, qk_ss, qk_rs, cam_ss, cam_rs, proto_ss, proto_rs, wide_ss, wide_rs,
 ):
@@ -211,45 +218,43 @@
     loop(0, PAIR, attend)
 
     class Exchange:
-        def __init__(self, order, peer, src, dst, send_sem, recv_sem):
-            self.order, self.peer, self.src, self.dst = order, peer, src, dst
+        def __init__(self, order, peer, src, slots, mine, send_sem, recv_sem):
+            self.order, self.peer, self.src, self.dst = order, peer, src, slots.at[mine]
             self.send_sem, self.recv_sem = send_sem, recv_sem
-
-        def copy(self, i, to):
-            return remote(self.src(to), self.dst, self.send_sem(i), self.recv_sem(i), to)
+            others = slots.at[pl.ds(0, len(order))]
+            self.whole = remote(others, others, send_sem, recv_sem, peer(order[0]))
 
         def start(self):
-            for i, o in enumerate(self.order):
-                self.copy(i, self.peer(o)).start()
+            for o in self.order:
+                to = self.peer(o)
+                remote(self.src(to), self.dst, self.send_sem, self.recv_sem, to).start()
 
         def landed(self):
-            to = self.peer(self.order[0])
-            loop(0, len(self.order), lambda i: self.copy(i, to).wait_recv())
+            self.whole.wait_recv()
 
         def left(self):
-            to = self.peer(self.order[0])
-            loop(0, len(self.order), lambda i: self.copy(i, to).wait_send())
-
-    def cam_exchange(k, src, dst):
-        return Exchange(CAM_ORDER, cam_peer, src, dst, lambda i: cam_ss.at[k, i], lambda i: cam_rs.at[k, i])
-
-    def wide_exchange(k, order, peer, src, dst):
-        return Exchange(
-            order, lambda o: peer(*o), src, dst, lambda i: wide_ss.at[k, i], lambda i: wide_rs.at[k, i]
-        )
-
-    w_out = cam_exchange(0, lambda to: w_send.at[to[0]], w_recv.at[cam])
-    pool_out = cam_exchange(1, lambda to: pool_send, pool_recv.at[cam])
-    mix_out = cam_exchange(2, lambda to: mix_send.at[to[0]], mix_recv.at[cam])
-    gz_out = cam_exchange(3, lambda to: gz_send, gz_recv.at[cam])
-    z_out = wide_exchange(0, CLIP_ORDER, yz_peer, lambda to: z_send, z_recv.at[clip])
-    side_out = wide_exchange(
-        1, CLIP_ORDER, yz_peer, lambda to: side_send.at[lax.div(to[1] * SHARE, LANES)], side_recv.at[clip]
-    )
-    gu_out = wide_exchange(2, R_ORDER, r_peer, lambda to: gu_send.at[to[0]], gu_recv.at[here])
+            self.whole.wait_send()
+
+    def cam_exchange(k, src, slots):
+        return Exchange(CAM_ORDER, cam_peer, src, slots, cam, cam_ss.at[k], cam_rs.at[k])
+
+    def clip_exchange(k, src, slots):
+        return Exchange(CLIP_ORDER, lambda o: yz_peer(*o), src, slots, clip, wide_ss.at[k], wide_rs.at[k])
+
+    def r_exchange(k, src, slots):
+        return Exchange(R_ORDER, lambda o: r_peer(*o), src, slots, here, wide_ss.at[k], wide_rs.at[k])
+
+    w_out = cam_exchange(0, lambda to: w_send.at[to[0]], w_recv)
+    pool_out = cam_exchange(1, lambda to: pool_send, pool_recv)
+    mix_out = cam_exchange(2, lambda to: mix_send.at[to[0]], mix_recv)
+    gz_out = cam_exchange(3, lambda to: gz_send, gz_recv)
+    z_out = clip_exchange(0, lambda to: z_send, z_recv)
+    side_out = clip_exchange(1, lambda to: side_send.at[lax.div(to[1] * SHARE, LANES)], side_recv)
+    gu_out = r_exchange(2, lambda to: gu_send.at[to[0]], gu_recv)
+    gs_out = r_exchange(6, lambda to: gs_send.at[to[0]], gs_recv)
 
     def row_exchange(step):
-        return wide_exchange(3 + step, R_ORDER, r_peer, lambda to: row_send.at[step], row_recv.at[step, here])
+        return r_exchange(3 + step, lambda to: row_send.at[step], row_recv.at[step])
 
     row_out = [row_exchange(step) for step in range(3)]
 
@@ -301,6 +306,16 @@
     z_out.start()
     z_recv[clip] = z_send[...]
 
+    def left(b):
+        loop(1, N_CAM, lambda o: k_copy(b, o).wait_send())
+        loop(0, PIECES, lambda part: loop(1, N_CAM, lambda o: q_copy(b, part, o).wait_send()))
+
+    loop(0, PAIR, left)
+    for i in range(N_Z - 1):
+        proto_copy(i).wait_send()
+    w_out.left()
+    pool_out.left()
+
     mix_out.landed()
     mix_sum = jnp.sum(mix_recv[...], axis=0)
     pooled_f = pooled.astype(F32)
@@ -312,8 +327,6 @@
     for i in range(N_Z - 1):
         proto_copy(i).wait_recv()
     z_out.landed()
-    side_out.start()
-    side_recv[clip] = side_send[lax.div(clip * SHARE, LANES)]
 
     embed = jnp.concatenate(
         [jnp.concatenate([z_recv[:, 2 * b + j, :] for j in range(2)], axis=1) for b in range(PAIR)], axis=0
@@ -324,11 +337,13 @@
     norm_buf[...] = jnp.broadcast_to(norm, norm_buf.shape)
     unit_b = unit.astype(BF16)
 
-    def total(step, sums):
+    def total(step, sums, meanwhile=None):
         tall = jnp.broadcast_to(jnp.sum(sums, axis=1, keepdims=True), (LANES, LANES))
         row_send[step] = tall.T[:1, :]
         row_out[step].start()
         row_recv[step, here] = row_send[step]
+        if meanwhile is not None:
+            meanwhile()
         row_out[step].landed()
         wide = jnp.sum(row_recv[step], axis=0)
         return jnp.broadcast_to(wide, (LANES, LANES)).T
@@ -345,38 +360,61 @@
         return rows + fold(scaled), probs + fold(exps)
 
     rows, probs = lax.fori_loop(0, N_Z, first, (zero, zero))
-    got = total(0, jnp.concatenate([rows, probs], axis=0))
+
+    def spread_rows(send, out, recv, value):
+        for p in range(N_CAM):
+            send[p] = value[p * 8 : (p + 1) * 8]
+        out.start()
+        recv[here] = send[cam]
+
+    empty = jnp.zeros((CLIPS, BOT), F32)
+
+    def while_waiting():
+        side_out.start()
+        side_recv[clip] = side_send[lax.div(clip * SHARE, LANES)]
+        soft = lax.fori_loop(0, N_Z, lambda s, sums: sums + split_dot(p_buf[s], proto_all[s]), empty)
+        spread_rows(gs_send, gs_out, gs_recv, soft)
+
+    got = total(0, jnp.concatenate([rows, probs], axis=0), while_waiting)
     row_scale = 1.0 / got[:CLIPS]
-    prob_scale = twice(1.0 / got[CLIPS:])
-    for step in (1, 2):
-        wide_scale = twice(row_scale)
-
-        def again(s, rows):
-            scores = a_buf[s]
-            scale = 1.0 / jnp.sum(scores * wide_scale, axis=0, keepdims=True)
-            v_buf[s] = jnp.broadcast_to(scale, (8, COLS))
-            return rows + fold(scores * scale)
-
-        rows = lax.fori_loop(0, N_Z, again, zero)
-        row_scale = 1.0 / total(step, jnp.concatenate([rows, rows], axis=0))[:CLIPS]
+    prob_scale = 1.0 / got[CLIPS:]
+    prob_buf[...] = prob_scale
+
+    def rescale(s, wide_scale):
+        scores = a_buf[s]
+        return scores * (1.0 / jnp.sum(scores * wide_scale, axis=0, keepdims=True))
+
     wide_scale = twice(row_scale)
-
-    def assigned(s):
-        return a_buf[s] * v_buf[s][0:1] * wide_scale
-
-    def grads(s, carry):
-        logit_grad = (PROTOS * (p_buf[s] * prob_scale - assigned(s))).astype(BF16)
-        g_buf[s] = logit_grad
-        return carry + dot(logit_grad, proto_all[s], NT)
-
-    grad_unit = lax.fori_loop(0, N_Z, grads, jnp.zeros((CLIPS, BOT), F32))
-    for p in range(N_CAM):
-        gu_send[p] = grad_unit[p * 8 : (p + 1) * 8]
-    gu_out.start()
-    gu_recv[here] = gu_send[cam]
-
-    codes_out[...] = PROTOS * assigned(z)
-    grad_proto = dot(unit_b, g_buf[z], TN)
+    rows = lax.fori_loop(0, N_Z, lambda s, sums: sums + fold(rescale(s, wide_scale)), zero)
+    row_scale = 1.0 / total(1, jnp.concatenate([rows, rows], axis=0))[:CLIPS]
+    last_scale = twice(row_scale)
+
+    def last(s, carry):
+        rows, sums = carry
+        scaled = rescale(s, last_scale)
+        a_buf[s] = scaled
+        return rows + fold(scaled), sums + split_dot(scaled, proto_all[s])
+
+    rows, hard = lax.fori_loop(0, N_Z, last, (zero, empty))
+    spread_rows(gu_send, gu_out, gu_recv, hard)
+    row_scale = 1.0 / total(2, jnp.concatenate([rows, rows], axis=0))[:CLIPS]
+    scale_buf[...] = row_scale
+
+    mine = pl.ds(pl.multiple_of(cam * 8, 8), 8)
+    gs_out.landed()
+    grad8 = jnp.sum(gs_recv[...], axis=0) * twice(prob_buf[mine, :])
+    gu_out.landed()
+    grad8 = PROTOS * (grad8 - jnp.sum(gu_recv[...], axis=0) * twice(scale_buf[mine, :]))
+    unit8 = unit_buf[mine, :]
+    grad8 = (grad8 - unit8 * jnp.sum(unit8 * grad8, axis=1, keepdims=True)) / norm_buf[mine, :]
+    gz_send[...] = grad8.astype(BF16).astype(F32)
+    gz_out.start()
+    gz_recv[cam] = gz_send[...]
+
+    assigned = a_buf[z] * twice(row_scale)
+    codes_out[...] = PROTOS * assigned
+    logit_grad = (PROTOS * (p_buf[z] * twice(prob_scale) - assigned)).astype(BF16)
+    grad_proto = dot(unit_b, logit_grad, TN)
     proto = pr[...].astype(F32)
     col_norm = jnp.sqrt(jnp.sum(proto * proto, axis=0, keepdims=True) + NORM_EPS)
     unit_proto = proto / col_norm
@@ -384,14 +422,6 @@
         grad_proto - unit_proto * jnp.sum(unit_proto * grad_proto, axis=0, keepdims=True)
     ) / col_norm
 
-    gu_out.landed()
-    grad8 = jnp.sum(gu_recv[...], axis=0)
-    mine = pl.ds(pl.multiple_of(cam * 8, 8), 8)
-    unit8 = unit_buf[mine, :]
-    grad8 = (grad8 - unit8 * jnp.sum(unit8 * grad8, axis=1, keepdims=True)) / norm_buf[mine, :]
-    gz_send[...] = grad8.astype(BF16).astype(F32)
-    gz_out.start()
-    gz_recv[cam] = gz_send[...]
     side_out.landed()
     pooled_all = jnp.concatenate([side_recv[:, b, :] for b in range(PAIR)], axis=0).astype(BF16)
     gz_out.landed()
@@ -411,14 +441,7 @@
     value_tmp[...] = jnp.where(lane < HD, by_head[0], by_head[1])
     value_out[...] = value_tmp[part, :]
 
-    def left(b):
-        loop(1, N_CAM, lambda o: k_copy(b, o).wait_send())
-        loop(0, PIECES, lambda part: loop(1, N_CAM, lambda o: q_copy(b, part, o).wait_send()))
-
-    loop(0, PAIR, left)
-    for i in range(N_Z - 1):
-        proto_copy(i).wait_send()
-    for out in [w_out, pool_out, mix_out, gz_out, z_out, side_out, gu_out] + row_out:
+    for out in [mix_out, gz_out, z_out, side_out, gs_out, gu_out] + row_out:
         out.left()
 
 
@@ -458,15 +481,16 @@
             vmem((PAIR * N_CAM, LANES), F32), vmem((N_CAM, PAIR * N_CAM, LANES), F32),
             vmem((4, LANES), F32), vmem((N_CLIP, 4, LANES), F32),
             vmem((N_CAM, 8, LANES), F32), vmem((N_CLIP, 8, LANES), F32),
-            vmem((N_Z, CLIPS, COLS), F32), vmem((N_Z, CLIPS, COLS), F32), vmem((N_Z, 8, COLS), F32),
-            vmem((N_Z, CLIPS, COLS), BF16), vmem((CLIPS, BOT), F32), vmem((CLIPS, BOT), F32),
+            vmem((N_Z, CLIPS, COLS), F32), vmem((N_Z, CLIPS, COLS), F32),
+            vmem((CLIPS, BOT), F32), vmem((CLIPS, BOT), F32), vmem((CLIPS, LANES), F32), vmem((CLIPS, LANES), F32),
             vmem((3, 1, LANES), F32), vmem((3, N_R, 1, LANES), F32),
+            vmem((N_CAM, 8, BOT), F32), vmem((N_R, 8, BOT), F32),
             vmem((N_CAM, 8, BOT), F32), vmem((N_R, 8, BOT), F32),
             vmem((8, BOT), F32), vmem((N_CAM, 8, BOT), F32),
             vmem((LANES, BOT), F32), vmem((LANES, LANES), F32),
             dma((7,)), dma((PAIR, PIECES + 1)), pltpu.SemaphoreType.REGULAR,
-            dma((PAIR, PIECES + 1, N_CAM)), dma((PAIR, PIECES + 1, N_CAM)), dma((4, N_CAM)), dma((4, N_CAM)),
-            dma((N_Z,)), dma((N_Z,)), dma((6, N_CLIP)), dma((6, N_CLIP)),
+            dma((PAIR, PIECES + 1, N_CAM)), dma((PAIR, PIECES + 1, N_CAM)), dma((4,)), dma((4,)),
+            dma((N_Z,)), dma((N_Z,)), dma((7,)), dma((7,)),
         ],
         compiler_params=pltpu.CompilerParams(
             collective_id=0, has_side_effects=True, vmem_limit_bytes=58 * 2**20

time: 93.6 us -> 83.4 us (0.89)
  Pallas kernels: 92.9 us -> 82.6 us
    pallas_call x1, Pallas kernels: 91.2 us -> 80.9 us  [local(): pl.pallas_call(kernel, out_shape=shapes, in_specs=[pl.BlockSpec(memory_sp...]
where the time goes in v3:
time: 83.4 us; the launch traced here: 83.3 us
  Pallas kernels  82.6 us (99%)
    pallas_call x1, Pallas kernels, local(): pl.pallas_call(kernel, out_shape=shapes, in_specs=[pl.BlockSpec(memory_sp...  80.9 us
    pallas_call x1, Pallas kernels, local(): pl.pallas_call(finish, out_shape=shapes, in_specs=[pl.BlockSpec(memory_sp...  1.7 us

profile of v3, /device:TPU:1, one launch (start us, length us, event | category | flops | bytes accessed | tf_op | source)
XLA Modules:
  0.0 83.3 jit_solution(5561844741351738554)
XLA Ops:
  0.6 80.9 %shard_map.93 = (f32[64,256]{1,0:T(8,128)}, f32[256,256]{1,0:T(8,128)}, f32[32,256]{1,0:T(8,128)}, f32[32,128]{1,0:T(8,128)}) custom-call(bf16[512,1024]{1,0:T(8,128)(2,1)} %bitcast.1, bf16[1024,1024]{1,0:T(8,128)(2,1)} %wq_in.1, bf16[1024,1024]{1,0:T(8,128)(2,1)} %wk_in.1, bf16[1024,1024]{1,0:T(8,128)(2,1)} %wv_in.1, bf16[1024,256]{1,0:T(8,128)(2,1)} %wp_in.1, ...), custom_call_target="tpu_custom_call" | custom-call | tf_op jit(solution)/shard_map/pallas_call | solution.py:467
  81.6 1.7 %shard_map.94 = (f32[64,256]{1,0:T(8,128)}, f32[256,256]{1,0:T(8,128)}, f32[32,256]{1,0:T(8,128)}, f32[32,128]{1,0:T(8,128)}) custom-call(f32[64,256]{1,0:T(8,128)} %get-tuple-element.8.codes, f32[256,256]{1,0:T(8,128)} %get-tuple-element.9.proto_grad, f32[32,256]{1,0:T(8,128)} %get-tuple-element.10.proj_grad, f32[32,128]{1,0:T(8,128)} %get-tuple-element.11.value_grad), custom_call_target="tpu_custom_call" | custom-call | tf_op jit(solution)/shard_map/pallas_call | solution.py:499

commit v4 on v3

--- a/solution.py
+++ b/solution.py
@@ -28,6 +28,8 @@
 PIECE = TOK // PIECES
 ROWS = N_CAM * PIECE
 
+VMEM_LIMIT = 58 * 2**20
+
 SINK_EPS = 0.05
 SOFTMAX_TEMP = 0.1
 NORM_EPS = 1e-06
@@ -78,7 +80,7 @@
     z_send, z_recv, side_send, side_recv,
     a_buf, p_buf, unit_buf, norm_buf, prob_buf, scale_buf,
     row_send, row_recv, gs_send, gs_recv, gu_send, gu_recv, gz_send, gz_recv,
-    proj_tmp, value_tmp,
+    side_tmp,
     load_sem, own_sem, y_sem, qk_ss, qk_rs, cam_ss, cam_rs, proto_ss, proto_rs, wide_ss, wide_rs,
 ):
     cam = lax.axis_index("cam")
@@ -86,14 +88,18 @@
     y, z = lax.div(clip, N_Z), lax.rem(clip, N_Z)
     here = y * N_CAM + cam
 
+    cams = [cam] + [lax.rem(cam + o, N_CAM) for o in range(1, N_CAM)]
+    lines = [lax.rem(y + o, N_Y) * N_Z for o in range(N_Y)]
+    depths = [z] + [lax.rem(z + o, N_Z) for o in range(1, N_Z)]
+
     def cam_peer(o):
-        return (lax.rem(cam + o, N_CAM), clip)
+        return (cams[o], clip)
 
     def yz_peer(oy, oz):
-        return (cam, lax.rem(y + oy, N_Y) * N_Z + lax.rem(z + oz, N_Z))
+        return (cam, lines[oy] + depths[oz])
 
     def r_peer(oy, oc):
-        return (lax.rem(cam + oc, N_CAM), lax.rem(y + oy, N_Y) * N_Z + z)
+        return (cams[oc], lines[oy] + z)
 
     def loop(lo, hi, step):
         def body(i, carry):
@@ -119,7 +125,7 @@
         pltpu.make_async_copy(wv_in, wv, load_sem.at[5]),
         pltpu.make_async_copy(wp_in, wp, load_sem.at[6]),
     ]
-    for load in loads:
+    for load in loads[:2]:
         load.start()
 
     def project_keys(b):
@@ -174,6 +180,8 @@
 
     loads[0].wait()
     loads[1].wait()
+    for load in loads[2:]:
+        load.start()
     project_keys(0)
     pl.semaphore_wait(barrier, N_CAM - 1 + N_Y - 1 + N_Z - 1)
     send_keys(0)
@@ -199,11 +207,13 @@
     lane_q = lax.broadcasted_iota(jnp.int32, (ROWS, LANES), 1)
 
     def attend(b):
-        loop(1, N_CAM, lambda o: k_copy(b, o).wait_recv())
+        for o in CAM_ORDER[::-1]:
+            k_copy(b, o).wait_recv()
         own_k(b).wait()
 
         def piece(part):
-            loop(1, N_CAM, lambda o: q_copy(b, part, o).wait_recv())
+            for o in CAM_ORDER[::-1]:
+                q_copy(b, part, o).wait_recv()
             own_q(b, part).wait()
             keys = k_recv[b].reshape(KEYS, LANES)
             both = q_recv[b, part].reshape(ROWS, LANES)
@@ -307,8 +317,14 @@
     z_recv[clip] = z_send[...]
 
     def left(b):
-        loop(1, N_CAM, lambda o: k_copy(b, o).wait_send())
-        loop(0, PIECES, lambda part: loop(1, N_CAM, lambda o: q_copy(b, part, o).wait_send()))
+        for o in CAM_ORDER:
+            k_copy(b, o).wait_send()
+
+        def part_left(part):
+            for o in CAM_ORDER:
+                q_copy(b, part, o).wait_send()
+
+        loop(0, PIECES, part_left)
 
     loop(0, PAIR, left)
     for i in range(N_Z - 1):
@@ -359,7 +375,7 @@
         scaled = scores * (1.0 / jnp.sum(scores, axis=0, keepdims=True))
         return rows + fold(scaled), probs + fold(exps)
 
-    rows, probs = lax.fori_loop(0, N_Z, first, (zero, zero))
+    rows, probs = lax.fori_loop(0, N_Z, first, (zero, zero), unroll=True)
 
     def spread_rows(send, out, recv, value):
         for p in range(N_CAM):
@@ -372,7 +388,7 @@
     def while_waiting():
         side_out.start()
         side_recv[clip] = side_send[lax.div(clip * SHARE, LANES)]
-        soft = lax.fori_loop(0, N_Z, lambda s, sums: sums + split_dot(p_buf[s], proto_all[s]), empty)
+        soft = lax.fori_loop(0, N_Z, lambda s, sums: sums + split_dot(p_buf[s], proto_all[s]), empty, unroll=True)
         spread_rows(gs_send, gs_out, gs_recv, soft)
 
     got = total(0, jnp.concatenate([rows, probs], axis=0), while_waiting)
@@ -385,7 +401,7 @@
         return scores * (1.0 / jnp.sum(scores * wide_scale, axis=0, keepdims=True))
 
     wide_scale = twice(row_scale)
-    rows = lax.fori_loop(0, N_Z, lambda s, sums: sums + fold(rescale(s, wide_scale)), zero)
+    rows = lax.fori_loop(0, N_Z, lambda s, sums: sums + fold(rescale(s, wide_scale)), zero, unroll=True)
     row_scale = 1.0 / total(1, jnp.concatenate([rows, rows], axis=0))[:CLIPS]
     last_scale = twice(row_scale)
 
@@ -395,7 +411,7 @@
         a_buf[s] = scaled
         return rows + fold(scaled), sums + split_dot(scaled, proto_all[s])
 
-    rows, hard = lax.fori_loop(0, N_Z, last, (zero, empty))
+    rows, hard = lax.fori_loop(0, N_Z, last, (zero, empty), unroll=True)
     spread_rows(gu_send, gu_out, gu_recv, hard)
     row_scale = 1.0 / total(2, jnp.concatenate([rows, rows], axis=0))[:CLIPS]
     scale_buf[...] = row_scale
@@ -423,23 +439,32 @@
     ) / col_norm
 
     side_out.landed()
-    pooled_all = jnp.concatenate([side_recv[:, b, :] for b in range(PAIR)], axis=0).astype(BF16)
+    part = pl.ds(pl.multiple_of(lax.rem(clip * SHARE, LANES), SHARE), SHARE)
+
+    def features(row):
+        tall = jnp.concatenate([side_recv[:, row(b), :] for b in range(PAIR)], axis=0).T
+        side_tmp[:, :CLIPS] = tall
+        return side_tmp[part, :][:, :CLIPS]
+
+    pooled_all = features(lambda b: b).astype(BF16)
+    parts = []
+    for head in range(PAIR):
+        mix_all = features(lambda b: 2 + PAIR * b + head)
+        high = mix_all.astype(BF16)
+        parts += [high, (mix_all - high.astype(F32)).astype(BF16)]
+    mix_parts = jnp.concatenate(parts, axis=0)
+
     gz_out.landed()
     grad_z = gz_recv[...].reshape(CLIPS, BOT).astype(BF16)
-
-    part = pl.ds(pl.multiple_of(lax.rem(clip * SHARE, LANES), SHARE), SHARE)
-    proj_tmp[...] = dot(pooled_all, grad_z, TN)
-    proj_out[...] = proj_tmp[part, :]
+    proj_out[...] = dot(pooled_all, grad_z, NN)
     grad_pooled = dot(grad_z, wp[pl.ds(pl.multiple_of(cam * LANES, LANES), LANES), :], NT).astype(BF16)
-    by_head = []
-    for head in range(PAIR):
-        mix_all = jnp.concatenate([side_recv[:, 2 + PAIR * b + head, :] for b in range(PAIR)], axis=0)
-        high = mix_all.astype(BF16)
-        low = (mix_all - high.astype(F32)).astype(BF16)
-        by_head.append(dot(high, grad_pooled, TN) + dot(low, grad_pooled, TN))
-    lane = lax.broadcasted_iota(jnp.int32, (LANES, LANES), 1)
-    value_tmp[...] = jnp.where(lane < HD, by_head[0], by_head[1])
-    value_out[...] = value_tmp[part, :]
+    by_head = dot(mix_parts, grad_pooled, NN)
+    lane = lax.broadcasted_iota(jnp.int32, (SHARE, LANES), 1)
+    value_out[...] = jnp.where(
+        lane < HD,
+        by_head[:SHARE] + by_head[SHARE : 2 * SHARE],
+        by_head[2 * SHARE : 3 * SHARE] + by_head[3 * SHARE :],
+    )
 
     for out in [mix_out, gz_out, z_out, side_out, gs_out, gu_out] + row_out:
         out.left()
@@ -487,13 +512,13 @@
             vmem((N_CAM, 8, BOT), F32), vmem((N_R, 8, BOT), F32),
             vmem((N_CAM, 8, BOT), F32), vmem((N_R, 8, BOT), F32),
             vmem((8, BOT), F32), vmem((N_CAM, 8, BOT), F32),
-            vmem((LANES, BOT), F32), vmem((LANES, LANES), F32),
+            vmem((LANES, LANES), F32),
             dma((7,)), dma((PAIR, PIECES + 1)), pltpu.SemaphoreType.REGULAR,
             dma((PAIR, PIECES + 1, N_CAM)), dma((PAIR, PIECES + 1, N_CAM)), dma((4,)), dma((4,)),
             dma((N_Z,)), dma((N_Z,)), dma((7,)), dma((7,)),
         ],
         compiler_params=pltpu.CompilerParams(
-            collective_id=0, has_side_effects=True, vmem_limit_bytes=58 * 2**20
+            collective_id=0, has_side_effects=True, vmem_limit_bytes=VMEM_LIMIT
         ),
     )(tokens.reshape(PAIR * TOK, D), w_query, w_key, w_value, w_proj, prototypes)
     return pl.pallas_call(

time: 83.4 us -> 81.9 us (0.982)
  Pallas kernels: 82.6 us -> 81.1 us
    pallas_call x1, Pallas kernels: 80.9 us -> 79.4 us  [local(): pl.pallas_call(kernel, out_shape=shapes, in_specs=[pl.BlockSpec(memory_sp...]
where the time goes in v4:
time: 81.9 us; the launch traced here: 81.8 us
  Pallas kernels  81.1 us (99%)
    pallas_call x1, Pallas kernels, local(): pl.pallas_call(kernel, out_shape=shapes, in_specs=[pl.BlockSpec(memory_sp...  79.4 us
    pallas_call x1, Pallas kernels, local(): pl.pallas_call(finish, out_shape=shapes, in_specs=[pl.BlockSpec(memory_sp...  1.7 us

profile of v4, /device:TPU:1, one launch (start us, length us, event | category | flops | bytes accessed | tf_op | source)
XLA Modules:
  0.0 81.8 jit_solution(8194925274479201851)
XLA Ops:
  0.6 79.4 %shard_map.93 = (f32[64,256]{1,0:T(8,128)}, f32[256,256]{1,0:T(8,128)}, f32[32,256]{1,0:T(8,128)}, f32[32,128]{1,0:T(8,128)}) custom-call(bf16[512,1024]{1,0:T(8,128)(2,1)} %bitcast.1, bf16[1024,1024]{1,0:T(8,128)(2,1)} %wq_in.1, bf16[1024,1024]{1,0:T(8,128)(2,1)} %wk_in.1, bf16[1024,1024]{1,0:T(8,128)(2,1)} %wv_in.1, bf16[1024,256]{1,0:T(8,128)(2,1)} %wp_in.1, ...), custom_call_target="tpu_custom_call" | custom-call | tf_op jit(solution)/shard_map/pallas_call | solution.py:492
  80.1 1.7 %shard_map.94 = (f32[64,256]{1,0:T(8,128)}, f32[256,256]{1,0:T(8,128)}, f32[32,256]{1,0:T(8,128)}, f32[32,128]{1,0:T(8,128)}) custom-call(f32[64,256]{1,0:T(8,128)} %get-tuple-element.8.codes, f32[256,256]{1,0:T(8,128)} %get-tuple-element.9.proto_grad, f32[32,256]{1,0:T(8,128)} %get-tuple-element.10.proj_grad, f32[32,128]{1,0:T(8,128)} %get-tuple-element.11.value_grad), custom_call_target="tpu_custom_call" | custom-call | tf_op jit(solution)/shard_map/pallas_call | solution.py:524

commit v5 on v4

--- a/solution.py
+++ b/solution.py
@@ -169,11 +169,10 @@
             k_copy(b, o).start()
         own_k(b).start()
 
-    def send_queries(b):
-        for part in range(PIECES):
-            for o in CAM_ORDER:
-                q_copy(b, part, o).start()
-            own_q(b, part).start()
+    def send_queries(b, part):
+        for o in CAM_ORDER:
+            q_copy(b, part, o).start()
+        own_q(b, part).start()
 
     def proto_copy(i):
         return remote(proto_all.at[z], proto_all.at[z], proto_ss.at[i], proto_rs.at[i], yz_peer(0, Z_ORDER[i]))
@@ -189,12 +188,11 @@
         pl.semaphore_signal(y_sem, inc=1, device_id=yz_peer(oy, 0), device_id_type=MESH)
     loads[2].wait()
     project_queries(0)
-    send_queries(0)
+    send_queries(0, 0)
+    send_queries(0, 1)
     loads[3].wait()
     project_keys(1)
-    send_keys(1)
     project_queries(1)
-    send_queries(1)
 
     loads[4].wait()
     proto = pr[...].astype(F32)
@@ -206,7 +204,7 @@
     acc[...] = jnp.zeros_like(acc)
     lane_q = lax.broadcasted_iota(jnp.int32, (ROWS, LANES), 1)
 
-    def attend(b):
+    def attend(b, sends):
         for o in CAM_ORDER[::-1]:
             k_copy(b, o).wait_recv()
         own_k(b).wait()
@@ -215,6 +213,13 @@
             for o in CAM_ORDER[::-1]:
                 q_copy(b, part, o).wait_recv()
             own_q(b, part).wait()
+            for at, blocks in sends.items():
+
+                @pl.when(part == at)
+                def _():
+                    for send in blocks:
+                        send()
+
             keys = k_recv[b].reshape(KEYS, LANES)
             both = q_recv[b, part].reshape(ROWS, LANES)
             for head in range(PAIR):
@@ -225,7 +230,11 @@
 
         loop(0, PIECES, piece)
 
-    loop(0, PAIR, attend)
+    def queries(b, part):
+        return functools.partial(send_queries, b, part)
+
+    attend(0, {0: (queries(0, 2), queries(0, 3)), 1: (functools.partial(send_keys, 1),), 3: (queries(1, 0),)})
+    attend(1, {0: (queries(1, 1), queries(1, 2)), 1: (queries(1, 3),)})
 
     class Exchange:
         def __init__(self, order, peer, src, slots, mine, send_sem, recv_sem):

time: 81.9 us -> 84.5 us (1.032)
  Pallas kernels: 81.1 us -> 83.7 us
    pallas_call x1, Pallas kernels: 79.4 us -> 82 us  [local(): pl.pallas_call(kernel, out_shape=shapes, in_specs=[pl.BlockSpec(memory_sp...]
where the time goes in v5:
time: 84.5 us; the launch traced here: 84.4 us
  Pallas kernels  83.7 us (99%)
    pallas_call x1, Pallas kernels, local(): pl.pallas_call(kernel, out_shape=shapes, in_specs=[pl.BlockSpec(memory_sp...  82 us
    pallas_call x1, Pallas kernels, local(): pl.pallas_call(finish, out_shape=shapes, in_specs=[pl.BlockSpec(memory_sp...  1.7 us

profile of v5, /device:TPU:1, one launch (start us, length us, event | category | flops | bytes accessed | tf_op | source)
XLA Modules:
  0.0 84.4 jit_solution(9259274747184282709)
XLA Ops:
  0.6 82.0 %shard_map.93 = (f32[64,256]{1,0:T(8,128)}, f32[256,256]{1,0:T(8,128)}, f32[32,256]{1,0:T(8,128)}, f32[32,128]{1,0:T(8,128)}) custom-call(bf16[512,1024]{1,0:T(8,128)(2,1)} %bitcast.1, bf16[1024,1024]{1,0:T(8,128)(2,1)} %wq_in.1, bf16[1024,1024]{1,0:T(8,128)(2,1)} %wk_in.1, bf16[1024,1024]{1,0:T(8,128)(2,1)} %wv_in.1, bf16[1024,256]{1,0:T(8,128)(2,1)} %wp_in.1, ...), custom_call_target="tpu_custom_call" | custom-call | tf_op jit(solution)/shard_map/pallas_call | solution.py:501
  82.7 1.7 %shard_map.94 = (f32[64,256]{1,0:T(8,128)}, f32[256,256]{1,0:T(8,128)}, f32[32,256]{1,0:T(8,128)}, f32[32,128]{1,0:T(8,128)}) custom-call(f32[64,256]{1,0:T(8,128)} %get-tuple-element.8.codes, f32[256,256]{1,0:T(8,128)} %get-tuple-element.9.proto_grad, f32[32,256]{1,0:T(8,128)} %get-tuple-element.10.proj_grad, f32[32,128]{1,0:T(8,128)} %get-tuple-element.11.value_grad), custom_call_target="tpu_custom_call" | custom-call | tf_op jit(solution)/shard_map/pallas_call | solution.py:533

commit v6 on v4

--- a/solution.py
+++ b/solution.py
@@ -24,7 +24,7 @@
 COLS = PROTOS // (N_CAM * N_CLIP)
 SHARE = D // N_CLIP
 KEYS = N_CAM * TOK
-PIECES = 4
+PIECES = 2
 PIECE = TOK // PIECES
 ROWS = N_CAM * PIECE
 
@@ -40,7 +40,7 @@
 BF16 = jnp.bfloat16
 
 
-CAM_ORDER = (4, 3, 5, 2, 6, 7, 1)
+CAM_ORDER = (4, 6, 2, 5, 3, 7, 1)
 Y_ORDER = (2, 1, 3, 0)
 Z_ORDER = (4, 3, 5, 2, 6, 1, 7, 0)
 CLIP_ORDER = tuple((oy, oz) for oy in Y_ORDER for oz in Z_ORDER if (oy, oz) != (0, 0))

time: 81.9 us -> 80.7 us (0.985)
  Pallas kernels: 81.1 us -> 79.9 us
    pallas_call x1, Pallas kernels: 79.4 us -> 78.2 us  [local(): pl.pallas_call(kernel, out_shape=shapes, in_specs=[pl.BlockSpec(memory_sp...]
where the time goes in v6:
time: 80.7 us; the launch traced here: 80.5 us
  Pallas kernels  79.9 us (99%)
    pallas_call x1, Pallas kernels, local(): pl.pallas_call(kernel, out_shape=shapes, in_specs=[pl.BlockSpec(memory_sp...  78.2 us
    pallas_call x1, Pallas kernels, local(): pl.pallas_call(finish, out_shape=shapes, in_specs=[pl.BlockSpec(memory_sp...  1.7 us

profile of v6, /device:TPU:1, one launch (start us, length us, event | category | flops | bytes accessed | tf_op | source)
XLA Modules:
  0.0 80.5 jit_solution(3965188175604177652)
XLA Ops:
  0.6 78.2 %shard_map.93 = (f32[64,256]{1,0:T(8,128)}, f32[256,256]{1,0:T(8,128)}, f32[32,256]{1,0:T(8,128)}, f32[32,128]{1,0:T(8,128)}) custom-call(bf16[512,1024]{1,0:T(8,128)(2,1)} %bitcast.1, bf16[1024,1024]{1,0:T(8,128)(2,1)} %wq_in.1, bf16[1024,1024]{1,0:T(8,128)(2,1)} %wk_in.1, bf16[1024,1024]{1,0:T(8,128)(2,1)} %wv_in.1, bf16[1024,256]{1,0:T(8,128)(2,1)} %wp_in.1, ...), custom_call_target="tpu_custom_call" | custom-call | tf_op jit(solution)/shard_map/pallas_call | solution.py:492
  78.8 1.7 %shard_map.94 = (f32[64,256]{1,0:T(8,128)}, f32[256,256]{1,0:T(8,128)}, f32[32,256]{1,0:T(8,128)}, f32[32,128]{1,0:T(8,128)}) custom-call(f32[64,256]{1,0:T(8,128)} %get-tuple-element.8.codes, f32[256,256]{1,0:T(8,128)} %get-tuple-element.9.proto_grad, f32[32,256]{1,0:T(8,128)} %get-tuple-element.10.proj_grad, f32[32,128]{1,0:T(8,128)} %get-tuple-element.11.value_grad), custom_call_target="tpu_custom_call" | custom-call | tf_op jit(solution)/shard_map/pallas_call | solution.py:524

commit v7 on v6

--- a/solution.py
+++ b/solution.py
@@ -24,7 +24,7 @@
 COLS = PROTOS // (N_CAM * N_CLIP)
 SHARE = D // N_CLIP
 KEYS = N_CAM * TOK
-PIECES = 2
+PIECES = 4
 PIECE = TOK // PIECES
 ROWS = N_CAM * PIECE
 

time: 80.7 us -> 80.7 us (level)
  no operation moved by 1% of the time
where the time goes in v7:
time: 80.7 us; the launch traced here: 80.5 us
  Pallas kernels  79.9 us (99%)
    pallas_call x1, Pallas kernels, local(): pl.pallas_call(kernel, out_shape=shapes, in_specs=[pl.BlockSpec(memory_sp...  78.2 us
    pallas_call x1, Pallas kernels, local(): pl.pallas_call(finish, out_shape=shapes, in_specs=[pl.BlockSpec(memory_sp...  1.7 us

profile of v7, /device:TPU:1, one launch (start us, length us, event | category | flops | bytes accessed | tf_op | source)
XLA Modules:
  0.0 80.5 jit_solution(8208289067439800346)
XLA Ops:
  0.6 78.2 %shard_map.93 = (f32[64,256]{1,0:T(8,128)}, f32[256,256]{1,0:T(8,128)}, f32[32,256]{1,0:T(8,128)}, f32[32,128]{1,0:T(8,128)}) custom-call(bf16[512,1024]{1,0:T(8,128)(2,1)} %bitcast.1, bf16[1024,1024]{1,0:T(8,128)(2,1)} %wq_in.1, bf16[1024,1024]{1,0:T(8,128)(2,1)} %wk_in.1, bf16[1024,1024]{1,0:T(8,128)(2,1)} %wv_in.1, bf16[1024,256]{1,0:T(8,128)(2,1)} %wp_in.1, ...), custom_call_target="tpu_custom_call" | custom-call | tf_op jit(solution)/shard_map/pallas_call | solution.py:492
  78.8 1.7 %shard_map.94 = (f32[64,256]{1,0:T(8,128)}, f32[256,256]{1,0:T(8,128)}, f32[32,256]{1,0:T(8,128)}, f32[32,128]{1,0:T(8,128)}) custom-call(f32[64,256]{1,0:T(8,128)} %get-tuple-element.8.codes, f32[256,256]{1,0:T(8,128)} %get-tuple-element.9.proto_grad, f32[32,256]{1,0:T(8,128)} %get-tuple-element.10.proj_grad, f32[32,128]{1,0:T(8,128)} %get-tuple-element.11.value_grad), custom_call_target="tpu_custom_call" | custom-call | tf_op jit(solution)/shard_map/pallas_call | solution.py:524
